TPU v7x, 256 devices: a whole 4x4x8 slice. The times are simulated.
256 devices in a mesh: seq: 32 (over z, x), head: 8 (over y, core).
Axes of the slice: x: 4, y: 4, z: 8, core: 2. Of those that a mesh axis runs over, the one named last changes fastest.
Arguments:
- queries: bfloat16 [32768, 4096], P('seq', 'head'), may hold values from -6 to 6
- key_vectors: bfloat16 [32768, 4096], P('seq', 'head'), may hold values from -6 to 6
- value_vectors: bfloat16 [32768, 4096], P('seq', 'head'), may hold values from -6 to 6
- gate_input: bfloat16 [32768, 4096], P('seq', 'head'), may hold values from -6 to 6
- log_decay: float32 [32768, 32], P('seq', 'head'), may hold values from -1.5 to 0, as said below
- out_weight: bfloat16 [4096, 4096], P('head'), may hold values from -0.09375 to 0.09375
Outputs:
- projected: bfloat16 [32768, 4096], P(('seq', 'head'))
Inputs may be any that keep to these rules, and one draw needn't show every extreme that they name: `log_decay`: every entry is negative.
All inputs are finite; a program needn't handle non-finite values.
Results may differ from a plain program's by a relative error of at most 0.0054.
Values sent between devices are 32-bit elements; how exact they have to be, the bound alone decides.
A program may use at most 128 MiB of HBM per device.

v0:
```python
import jax
import jax.numpy as jnp
from jax import lax
from jax.sharding import PartitionSpec as P

HEAD_DIM = 128
BLOCK_LEN = 256


def passed_along(block, axis, distance):
    devices = range(lax.axis_size(axis))
    route = [(i - distance, i) for i in devices if i - distance in devices]
    return lax.ppermute(block, axis, route)


def per_device(queries, key_vectors, value_vectors, gate_input, log_decay, out_weight):
    token_count, feature_count = queries.shape
    local_heads = feature_count // HEAD_DIM
    block_count = token_count // BLOCK_LEN
    split_shape = (block_count, BLOCK_LEN, local_heads, HEAD_DIM)
    highest = lax.Precision.HIGHEST
    query_blocks = queries.reshape(split_shape)
    key_blocks = key_vectors.reshape(split_shape)
    value_blocks = value_vectors.reshape(split_shape)
    log_rates = log_decay.reshape(block_count, BLOCK_LEN, local_heads)
    running = jnp.cumsum(log_rates, axis=1)
    block_total = running[:, -1, :]
    scores = jnp.einsum(
        "cihd,cjhd->chij", query_blocks, key_blocks, preferred_element_type=jnp.float32
    )
    token_places = lax.iota(jnp.int32, BLOCK_LEN)
    causal = token_places[:, None] >= token_places[None, :]
    by_head = jnp.transpose(running, (0, 2, 1))
    spread = by_head[:, :, :, None] - by_head[:, :, None, :]
    decay = jnp.exp(jnp.where(causal, spread, -1e30))
    weights = (scores * decay).astype(jnp.bfloat16)
    inside = jnp.einsum(
        "chij,cjhd->cihd", weights, value_blocks, preferred_element_type=jnp.float32
    )
    query_scaled = query_blocks.astype(jnp.float32) * jnp.exp(running)[..., None]
    key_scaled = (
        key_blocks.astype(jnp.float32) * jnp.exp(block_total[:, None, :] - running)[..., None]
    )
    contribution = jnp.einsum(
        "cjhd,cjhe->chde", key_scaled, value_blocks.astype(jnp.float32), precision=highest
    )
    block_decay = jnp.exp(block_total)
    lead_decay = jnp.exp(jnp.cumsum(block_total, axis=0) - block_total)
    start_list = []
    running_state = jnp.zeros((local_heads, HEAD_DIM, HEAD_DIM), jnp.float32)
    for block_index in range(block_count):
        start_list.append(running_state)
        running_state = (
            block_decay[block_index][:, None, None] * running_state + contribution[block_index]
        )
    start_states = jnp.stack(start_list)
    end_state = running_state
    through = jnp.exp(jnp.sum(block_total, axis=0))

    def relay_turn(turn_index, passed):
        return passed_along(through[:, None, None] * passed + end_state, "seq", 1)

    incoming = lax.fori_loop(0, lax.axis_size("seq") - 1, relay_turn, jnp.zeros_like(end_state))
    combined = start_states + lead_decay[:, :, None, None] * incoming[None]
    carried = jnp.einsum("cihd,chde->cihe", query_scaled, combined, precision=highest)
    attended = (inside + carried).reshape(token_count, local_heads, HEAD_DIM)
    inverse_rms = lax.rsqrt(jnp.mean(attended * attended, axis=-1, keepdims=True) + 1e-06)
    normed = (attended * inverse_rms).reshape(token_count, feature_count)
    hidden = (normed * jax.nn.silu(gate_input.astype(jnp.float32))).astype(jnp.bfloat16)
    return lax.psum_scatter(
        jnp.dot(hidden, out_weight, preferred_element_type=jnp.float32),
        "head",
        scatter_dimension=0,
        tiled=True,
    ).astype(jnp.bfloat16)


def solution(mesh):
    placed = (
        P("seq", "head"),
        P("seq", "head"),
        P("seq", "head"),
        P("seq", "head"),
        P("seq", "head"),
        P("head", None),
    )
    return jax.shard_map(
        per_device, mesh=mesh, in_specs=placed, out_specs=P(("seq", "head"), None), check_vma=False
    )
```

profile of v0, /device:TPU:1, one launch (start us, length us, event | category | flops | bytes accessed | tf_op | source)
XLA Modules:
  0.0 532.5 jit_solution(11855316472746125915)
XLA Ops:
  7.4 4.8 reduce-window.6
  20.9 4.3 fusion.13
  25.2 306.6 %while.10 = (s32[]{:T(128)}, f32[4,128,128]{2,1,0:T(8,128)S(1)}, f32[4]{0:T(128)S(1)}, f32[4,128,128]{2,1,0:T(8,128)S(1)}, s32[]{:T(128)}) while((s32[]{:T(128)}, f32[4,128,128]{2,1,0:T(8,128)S(1)}, f32[4]{0:T(128)S(1)}, f32[4,128,128]{2,1,0:T(8,128)S(1)}, s32[]{:T(128)}) %tuple.27), condition=%wide.region_5.6_spmd, body=%wide.region_4.5_spmd.sunk | while | flops 131074 | bytes 1835125 | solution.py:63
  25.4 4.1 collective-permute-start
  29.4 4.9 collective-permute-done
  34.5 4.1 collective-permute-start
  38.6 4.1 collective-permute-done
  42.8 4.1 collective-permute-start
  46.9 3.3 collective-permute-done
  50.3 3.8 collective-permute-start
  54.1 3.3 collective-permute-done
  57.5 3.8 collective-permute-start
  61.3 3.3 collective-permute-done
  64.7 6.1 %collective-permute-start = (f32[4,128,128]{2,1,0:T(8,128)S(1)}, f32[4,128,128]{2,1,0:T(8,128)S(1)}, u32[]{:S(2)}, u32[]{:S(2)}) collective-permute-start(f32[4,128,128]{2,1,0:T(8,128)S(1)} %multiply_add_fusion.5), channel_id=1, source_target_pairs={{0,8},{8,16},{16,24},{24,32},{32,40},{40,48},{48,56},{56,64},{64,7... | collective-permute-start | bytes 786440 | tf_op jit(solution)/shard_map/while/body/eval_jaxpr/ppermute | solution.py:13
  70.8 3.3 collective-permute-done
  74.2 5.9 %collective-permute-start = (f32[4,128,128]{2,1,0:T(8,128)S(1)}, f32[4,128,128]{2,1,0:T(8,128)S(1)}, u32[]{:S(2)}, u32[]{:S(2)}) collective-permute-start(f32[4,128,128]{2,1,0:T(8,128)S(1)} %multiply_add_fusion.5), channel_id=1, source_target_pairs={{0,8},{8,16},{16,24},{24,32},{32,40},{40,48},{48,56},{56,64},{64,7... | collective-permute-start | bytes 786440 | tf_op jit(solution)/shard_map/while/body/eval_jaxpr/ppermute | solution.py:13
  80.1 3.3 collective-permute-done
  83.5 5.9 %collective-permute-start = (f32[4,128,128]{2,1,0:T(8,128)S(1)}, f32[4,128,128]{2,1,0:T(8,128)S(1)}, u32[]{:S(2)}, u32[]{:S(2)}) collective-permute-start(f32[4,128,128]{2,1,0:T(8,128)S(1)} %multiply_add_fusion.5), channel_id=1, source_target_pairs={{0,8},{8,16},{16,24},{24,32},{32,40},{40,48},{48,56},{56,64},{64,7... | collective-permute-start | bytes 786440 | tf_op jit(solution)/shard_map/while/body/eval_jaxpr/ppermute | solution.py:13
  89.4 3.3 collective-permute-done
  92.8 6.2 %collective-permute-start = (f32[4,128,128]{2,1,0:T(8,128)S(1)}, f32[4,128,128]{2,1,0:T(8,128)S(1)}, u32[]{:S(2)}, u32[]{:S(2)}) collective-permute-start(f32[4,128,128]{2,1,0:T(8,128)S(1)} %multiply_add_fusion.5), channel_id=1, source_target_pairs={{0,8},{8,16},{16,24},{24,32},{32,40},{40,48},{48,56},{56,64},{64,7... | collective-permute-start | bytes 786440 | tf_op jit(solution)/shard_map/while/body/eval_jaxpr/ppermute | solution.py:13
  99.1 4.5 collective-permute-done
  103.6 6.5 %collective-permute-start = (f32[4,128,128]{2,1,0:T(8,128)S(1)}, f32[4,128,128]{2,1,0:T(8,128)S(1)}, u32[]{:S(2)}, u32[]{:S(2)}) collective-permute-start(f32[4,128,128]{2,1,0:T(8,128)S(1)} %multiply_add_fusion.5), channel_id=1, source_target_pairs={{0,8},{8,16},{16,24},{24,32},{32,40},{40,48},{48,56},{56,64},{64,7... | collective-permute-start | bytes 786440 | tf_op jit(solution)/shard_map/while/body/eval_jaxpr/ppermute | solution.py:13
  110.2 5.6 %collective-permute-done = f32[4,128,128]{2,1,0:T(8,128)S(1)} collective-permute-done((f32[4,128,128]{2,1,0:T(8,128)S(1)}, f32[4,128,128]{2,1,0:T(8,128)S(1)}, u32[]{:S(2)}, u32[]{:S(2)}) %collective-permute-start) | collective-permute-done | bytes 262176 | tf_op jit(solution)/shard_map/while/body/eval_jaxpr/ppermute | solution.py:13
  115.9 6.8 %collective-permute-start = (f32[4,128,128]{2,1,0:T(8,128)S(1)}, f32[4,128,128]{2,1,0:T(8,128)S(1)}, u32[]{:S(2)}, u32[]{:S(2)}) collective-permute-start(f32[4,128,128]{2,1,0:T(8,128)S(1)} %multiply_add_fusion.5), channel_id=1, source_target_pairs={{0,8},{8,16},{16,24},{24,32},{32,40},{40,48},{48,56},{56,64},{64,7... | collective-permute-start | bytes 786440 | tf_op jit(solution)/shard_map/while/body/eval_jaxpr/ppermute | solution.py:13
  122.7 5.4 %collective-permute-done = f32[4,128,128]{2,1,0:T(8,128)S(1)} collective-permute-done((f32[4,128,128]{2,1,0:T(8,128)S(1)}, f32[4,128,128]{2,1,0:T(8,128)S(1)}, u32[]{:S(2)}, u32[]{:S(2)}) %collective-permute-start) | collective-permute-done | bytes 262176 | tf_op jit(solution)/shard_map/while/body/eval_jaxpr/ppermute | solution.py:13
  128.2 6.0 %collective-permute-start = (f32[4,128,128]{2,1,0:T(8,128)S(1)}, f32[4,128,128]{2,1,0:T(8,128)S(1)}, u32[]{:S(2)}, u32[]{:S(2)}) collective-permute-start(f32[4,128,128]{2,1,0:T(8,128)S(1)} %multiply_add_fusion.5), channel_id=1, source_target_pairs={{0,8},{8,16},{16,24},{24,32},{32,40},{40,48},{48,56},{56,64},{64,7... | collective-permute-start | bytes 786440 | tf_op jit(solution)/shard_map/while/body/eval_jaxpr/ppermute | solution.py:13
  134.3 4.3 collective-permute-done
  138.6 5.0 collective-permute-start
  147.1 6.2 %collective-permute-start = (f32[4,128,128]{2,1,0:T(8,128)S(1)}, f32[4,128,128]{2,1,0:T(8,128)S(1)}, u32[]{:S(2)}, u32[]{:S(2)}) collective-permute-start(f32[4,128,128]{2,1,0:T(8,128)S(1)} %multiply_add_fusion.5), channel_id=1, source_target_pairs={{0,8},{8,16},{16,24},{24,32},{32,40},{40,48},{48,56},{56,64},{64,7... | collective-permute-start | bytes 786440 | tf_op jit(solution)/shard_map/while/body/eval_jaxpr/ppermute | solution.py:13
  153.3 3.3 collective-permute-done
  156.7 6.2 %collective-permute-start = (f32[4,128,128]{2,1,0:T(8,128)S(1)}, f32[4,128,128]{2,1,0:T(8,128)S(1)}, u32[]{:S(2)}, u32[]{:S(2)}) collective-permute-start(f32[4,128,128]{2,1,0:T(8,128)S(1)} %multiply_add_fusion.5), channel_id=1, source_target_pairs={{0,8},{8,16},{16,24},{24,32},{32,40},{40,48},{48,56},{56,64},{64,7... | collective-permute-start | bytes 786440 | tf_op jit(solution)/shard_map/while/body/eval_jaxpr/ppermute | solution.py:13
  162.9 3.3 collective-permute-done
  166.3 6.2 %collective-permute-start = (f32[4,128,128]{2,1,0:T(8,128)S(1)}, f32[4,128,128]{2,1,0:T(8,128)S(1)}, u32[]{:S(2)}, u32[]{:S(2)}) collective-permute-start(f32[4,128,128]{2,1,0:T(8,128)S(1)} %multiply_add_fusion.5), channel_id=1, source_target_pairs={{0,8},{8,16},{16,24},{24,32},{32,40},{40,48},{48,56},{56,64},{64,7... | collective-permute-start | bytes 786440 | tf_op jit(solution)/shard_map/while/body/eval_jaxpr/ppermute | solution.py:13
  172.5 3.3 collective-permute-done
  175.9 5.9 %collective-permute-start = (f32[4,128,128]{2,1,0:T(8,128)S(1)}, f32[4,128,128]{2,1,0:T(8,128)S(1)}, u32[]{:S(2)}, u32[]{:S(2)}) collective-permute-start(f32[4,128,128]{2,1,0:T(8,128)S(1)} %multiply_add_fusion.5), channel_id=1, source_target_pairs={{0,8},{8,16},{16,24},{24,32},{32,40},{40,48},{48,56},{56,64},{64,7... | collective-permute-start | bytes 786440 | tf_op jit(solution)/shard_map/while/body/eval_jaxpr/ppermute | solution.py:13
  181.8 3.3 collective-permute-done
  185.2 5.9 %collective-permute-start = (f32[4,128,128]{2,1,0:T(8,128)S(1)}, f32[4,128,128]{2,1,0:T(8,128)S(1)}, u32[]{:S(2)}, u32[]{:S(2)}) collective-permute-start(f32[4,128,128]{2,1,0:T(8,128)S(1)} %multiply_add_fusion.5), channel_id=1, source_target_pairs={{0,8},{8,16},{16,24},{24,32},{32,40},{40,48},{48,56},{56,64},{64,7... | collective-permute-start | bytes 786440 | tf_op jit(solution)/shard_map/while/body/eval_jaxpr/ppermute | solution.py:13
  191.2 3.4 collective-permute-done
  194.7 6.2 %collective-permute-start = (f32[4,128,128]{2,1,0:T(8,128)S(1)}, f32[4,128,128]{2,1,0:T(8,128)S(1)}, u32[]{:S(2)}, u32[]{:S(2)}) collective-permute-start(f32[4,128,128]{2,1,0:T(8,128)S(1)} %multiply_add_fusion.5), channel_id=1, source_target_pairs={{0,8},{8,16},{16,24},{24,32},{32,40},{40,48},{48,56},{56,64},{64,7... | collective-permute-start | bytes 786440 | tf_op jit(solution)/shard_map/while/body/eval_jaxpr/ppermute | solution.py:13
  201.0 4.6 collective-permute-done
  205.6 6.5 %collective-permute-start = (f32[4,128,128]{2,1,0:T(8,128)S(1)}, f32[4,128,128]{2,1,0:T(8,128)S(1)}, u32[]{:S(2)}, u32[]{:S(2)}) collective-permute-start(f32[4,128,128]{2,1,0:T(8,128)S(1)} %multiply_add_fusion.5), channel_id=1, source_target_pairs={{0,8},{8,16},{16,24},{24,32},{32,40},{40,48},{48,56},{56,64},{64,7... | collective-permute-start | bytes 786440 | tf_op jit(solution)/shard_map/while/body/eval_jaxpr/ppermute | solution.py:13
  212.2 5.7 %collective-permute-done = f32[4,128,128]{2,1,0:T(8,128)S(1)} collective-permute-done((f32[4,128,128]{2,1,0:T(8,128)S(1)}, f32[4,128,128]{2,1,0:T(8,128)S(1)}, u32[]{:S(2)}, u32[]{:S(2)}) %collective-permute-start) | collective-permute-done | bytes 262176 | tf_op jit(solution)/shard_map/while/body/eval_jaxpr/ppermute | solution.py:13
  218.0 6.9 %collective-permute-start = (f32[4,128,128]{2,1,0:T(8,128)S(1)}, f32[4,128,128]{2,1,0:T(8,128)S(1)}, u32[]{:S(2)}, u32[]{:S(2)}) collective-permute-start(f32[4,128,128]{2,1,0:T(8,128)S(1)} %multiply_add_fusion.5), channel_id=1, source_target_pairs={{0,8},{8,16},{16,24},{24,32},{32,40},{40,48},{48,56},{56,64},{64,7... | collective-permute-start | bytes 786440 | tf_op jit(solution)/shard_map/while/body/eval_jaxpr/ppermute | solution.py:13
  224.9 5.3 %collective-permute-done = f32[4,128,128]{2,1,0:T(8,128)S(1)} collective-permute-done((f32[4,128,128]{2,1,0:T(8,128)S(1)}, f32[4,128,128]{2,1,0:T(8,128)S(1)}, u32[]{:S(2)}, u32[]{:S(2)}) %collective-permute-start) | collective-permute-done | bytes 262176 | tf_op jit(solution)/shard_map/while/body/eval_jaxpr/ppermute | solution.py:13
  230.3 5.6 %collective-permute-start = (f32[4,128,128]{2,1,0:T(8,128)S(1)}, f32[4,128,128]{2,1,0:T(8,128)S(1)}, u32[]{:S(2)}, u32[]{:S(2)}) collective-permute-start(f32[4,128,128]{2,1,0:T(8,128)S(1)} %multiply_add_fusion.5), channel_id=1, source_target_pairs={{0,8},{8,16},{16,24},{24,32},{32,40},{40,48},{48,56},{56,64},{64,7... | collective-permute-start | bytes 786440 | tf_op jit(solution)/shard_map/while/body/eval_jaxpr/ppermute | solution.py:13
  236.0 4.1 collective-permute-done
  240.2 5.0 collective-permute-start
  245.3 3.3 collective-permute-done
  248.6 6.2 %collective-permute-start = (f32[4,128,128]{2,1,0:T(8,128)S(1)}, f32[4,128,128]{2,1,0:T(8,128)S(1)}, u32[]{:S(2)}, u32[]{:S(2)}) collective-permute-start(f32[4,128,128]{2,1,0:T(8,128)S(1)} %multiply_add_fusion.5), channel_id=1, source_target_pairs={{0,8},{8,16},{16,24},{24,32},{32,40},{40,48},{48,56},{56,64},{64,7... | collective-permute-start | bytes 786440 | tf_op jit(solution)/shard_map/while/body/eval_jaxpr/ppermute | solution.py:13
  258.3 6.2 %collective-permute-start = (f32[4,128,128]{2,1,0:T(8,128)S(1)}, f32[4,128,128]{2,1,0:T(8,128)S(1)}, u32[]{:S(2)}, u32[]{:S(2)}) collective-permute-start(f32[4,128,128]{2,1,0:T(8,128)S(1)} %multiply_add_fusion.5), channel_id=1, source_target_pairs={{0,8},{8,16},{16,24},{24,32},{32,40},{40,48},{48,56},{56,64},{64,7... | collective-permute-start | bytes 786440 | tf_op jit(solution)/shard_map/while/body/eval_jaxpr/ppermute | solution.py:13
  264.5 3.3 collective-permute-done
  267.9 6.2 %collective-permute-start = (f32[4,128,128]{2,1,0:T(8,128)S(1)}, f32[4,128,128]{2,1,0:T(8,128)S(1)}, u32[]{:S(2)}, u32[]{:S(2)}) collective-permute-start(f32[4,128,128]{2,1,0:T(8,128)S(1)} %multiply_add_fusion.5), channel_id=1, source_target_pairs={{0,8},{8,16},{16,24},{24,32},{32,40},{40,48},{48,56},{56,64},{64,7... | collective-permute-start | bytes 786440 | tf_op jit(solution)/shard_map/while/body/eval_jaxpr/ppermute | solution.py:13
  277.5 5.9 %collective-permute-start = (f32[4,128,128]{2,1,0:T(8,128)S(1)}, f32[4,128,128]{2,1,0:T(8,128)S(1)}, u32[]{:S(2)}, u32[]{:S(2)}) collective-permute-start(f32[4,128,128]{2,1,0:T(8,128)S(1)} %multiply_add_fusion.5), channel_id=1, source_target_pairs={{0,8},{8,16},{16,24},{24,32},{32,40},{40,48},{48,56},{56,64},{64,7... | collective-permute-start | bytes 786440 | tf_op jit(solution)/shard_map/while/body/eval_jaxpr/ppermute | solution.py:13
  286.8 5.9 %collective-permute-start = (f32[4,128,128]{2,1,0:T(8,128)S(1)}, f32[4,128,128]{2,1,0:T(8,128)S(1)}, u32[]{:S(2)}, u32[]{:S(2)}) collective-permute-start(f32[4,128,128]{2,1,0:T(8,128)S(1)} %multiply_add_fusion.5), channel_id=1, source_target_pairs={{0,8},{8,16},{16,24},{24,32},{32,40},{40,48},{48,56},{56,64},{64,7... | collective-permute-start | bytes 786440 | tf_op jit(solution)/shard_map/while/body/eval_jaxpr/ppermute | solution.py:13
  292.8 3.6 collective-permute-done
  296.4 6.2 %collective-permute-start = (f32[4,128,128]{2,1,0:T(8,128)S(1)}, f32[4,128,128]{2,1,0:T(8,128)S(1)}, u32[]{:S(2)}, u32[]{:S(2)}) collective-permute-start(f32[4,128,128]{2,1,0:T(8,128)S(1)} %multiply_add_fusion.5), channel_id=1, source_target_pairs={{0,8},{8,16},{16,24},{24,32},{32,40},{40,48},{48,56},{56,64},{64,7... | collective-permute-start | bytes 786440 | tf_op jit(solution)/shard_map/while/body/eval_jaxpr/ppermute | solution.py:13
  302.7 4.7 collective-permute-done
  307.5 6.5 %collective-permute-start = (f32[4,128,128]{2,1,0:T(8,128)S(1)}, f32[4,128,128]{2,1,0:T(8,128)S(1)}, u32[]{:S(2)}, u32[]{:S(2)}) collective-permute-start(f32[4,128,128]{2,1,0:T(8,128)S(1)} %multiply_add_fusion.5), channel_id=1, source_target_pairs={{0,8},{8,16},{16,24},{24,32},{32,40},{40,48},{48,56},{56,64},{64,7... | collective-permute-start | bytes 786440 | tf_op jit(solution)/shard_map/while/body/eval_jaxpr/ppermute | solution.py:13
  314.0 5.8 %collective-permute-done = f32[4,128,128]{2,1,0:T(8,128)S(1)} collective-permute-done((f32[4,128,128]{2,1,0:T(8,128)S(1)}, f32[4,128,128]{2,1,0:T(8,128)S(1)}, u32[]{:S(2)}, u32[]{:S(2)}) %collective-permute-start) | collective-permute-done | bytes 262176 | tf_op jit(solution)/shard_map/while/body/eval_jaxpr/ppermute | solution.py:13
  319.9 6.8 %collective-permute-start = (f32[4,128,128]{2,1,0:T(8,128)S(1)}, f32[4,128,128]{2,1,0:T(8,128)S(1)}, u32[]{:S(2)}, u32[]{:S(2)}) collective-permute-start(f32[4,128,128]{2,1,0:T(8,128)S(1)} %multiply_add_fusion.5), channel_id=1, source_target_pairs={{0,8},{8,16},{16,24},{24,32},{32,40},{40,48},{48,56},{56,64},{64,7... | collective-permute-start | bytes 786440 | tf_op jit(solution)/shard_map/while/body/eval_jaxpr/ppermute | solution.py:13
  326.7 5.1 collective-permute-done
  331.9 4.7 multiply_reduce_fusion
  340.3 12.9 %fusion.14 = f32[1024,4096]{1,0:T(8,128)} fusion(bf16[512,4096]{1,0:T(8,128)(2,1)} %param.13, bf16[1024,512]{1,0:T(8,128)(2,1)} %param.11, f32[128,8,4,128]{3,2,1,0:T(4,128)S(1)} %bitcast.64, f32[128,8,4,128]{3,2,1,0:T(4,128)S(1)} %bitcast.65), kind=kOutput, calls=%fused_computation.19 | convolution fusion | flops 4299161600 | bytes 26214400 | tf_op jit(solution)/shard_map/dot_general | solution.py:71
  353.2 169.7 %reduce-scatter.2.cloned.1.call-done = f32[128,4096]{1,0:T(8,128)} async-done(((f32[1024,4096]{1,0:T(8,128)}), f32[128,4096]{1,0:T(8,128)}) %reduce-scatter.2.cloned.1.call-update) | async-done | bytes 2097168 | tf_op jit(solution)/shard_map/reduce_scatter | solution.py:70
  (76 shorter events, 31.8 us)
Async XLA Ops:
  6.5 8.8 %copy-start.2 = (bf16[1024,512]{1,0:T(8,128)(2,1)S(1)}, bf16[1024,512]{1,0:T(8,128)(2,1)}, u32[]{:S(2)}) copy-start(bf16[1024,512]{1,0:T(8,128)(2,1)} %param.10) | copy-start | bytes 3145732
  6.5 516.4 %reduce-scatter.2.cloned.1.call-start = ((), (), s32[]{:S(2)}) async-start(), calls=%async_computation.1 | async-start | bytes 18874368 | tf_op jit(solution)/shard_map/reduce_scatter | solution.py:70
  13.1 2.5 copy-start.3
  25.2 306.7 %copy-start = (bf16[4,256,4,128]{3,2,1,0:T(4,128)(2,1)S(1)}, bf16[4,256,4,128]{3,2,1,0:T(4,128)(2,1)}, u32[]{:S(2)}) copy-start(bf16[4,256,4,128]{3,2,1,0:T(4,128)(2,1)} %reshape.89) | copy-start | bytes 3145732
  25.4 9.0 %collective-permute-start = (f32[4,128,128]{2,1,0:T(8,128)S(1)}, f32[4,128,128]{2,1,0:T(8,128)S(1)}, u32[]{:S(2)}, u32[]{:S(2)}) collective-permute-start(f32[4,128,128]{2,1,0:T(8,128)S(1)} %multiply_add_fusion.5), channel_id=1, source_target_pairs={{0,8},{8,16},{16,24},{24,32},{32,40},{40,48},{48,56},{56,64},{64,7... | collective-permute-start | bytes 786440 | tf_op jit(solution)/shard_map/while/body/eval_jaxpr/ppermute | solution.py:13
  34.5 8.2 %collective-permute-start = (f32[4,128,128]{2,1,0:T(8,128)S(1)}, f32[4,128,128]{2,1,0:T(8,128)S(1)}, u32[]{:S(2)}, u32[]{:S(2)}) collective-permute-start(f32[4,128,128]{2,1,0:T(8,128)S(1)} %multiply_add_fusion.5), channel_id=1, source_target_pairs={{0,8},{8,16},{16,24},{24,32},{32,40},{40,48},{48,56},{56,64},{64,7... | collective-permute-start | bytes 786440 | tf_op jit(solution)/shard_map/while/body/eval_jaxpr/ppermute | solution.py:13
  42.8 7.4 %collective-permute-start = (f32[4,128,128]{2,1,0:T(8,128)S(1)}, f32[4,128,128]{2,1,0:T(8,128)S(1)}, u32[]{:S(2)}, u32[]{:S(2)}) collective-permute-start(f32[4,128,128]{2,1,0:T(8,128)S(1)} %multiply_add_fusion.5), channel_id=1, source_target_pairs={{0,8},{8,16},{16,24},{24,32},{32,40},{40,48},{48,56},{56,64},{64,7... | collective-permute-start | bytes 786440 | tf_op jit(solution)/shard_map/while/body/eval_jaxpr/ppermute | solution.py:13
  50.3 7.1 %collective-permute-start = (f32[4,128,128]{2,1,0:T(8,128)S(1)}, f32[4,128,128]{2,1,0:T(8,128)S(1)}, u32[]{:S(2)}, u32[]{:S(2)}) collective-permute-start(f32[4,128,128]{2,1,0:T(8,128)S(1)} %multiply_add_fusion.5), channel_id=1, source_target_pairs={{0,8},{8,16},{16,24},{24,32},{32,40},{40,48},{48,56},{56,64},{64,7... | collective-permute-start | bytes 786440 | tf_op jit(solution)/shard_map/while/body/eval_jaxpr/ppermute | solution.py:13
  57.5 7.1 %collective-permute-start = (f32[4,128,128]{2,1,0:T(8,128)S(1)}, f32[4,128,128]{2,1,0:T(8,128)S(1)}, u32[]{:S(2)}, u32[]{:S(2)}) collective-permute-start(f32[4,128,128]{2,1,0:T(8,128)S(1)} %multiply_add_fusion.5), channel_id=1, source_target_pairs={{0,8},{8,16},{16,24},{24,32},{32,40},{40,48},{48,56},{56,64},{64,7... | collective-permute-start | bytes 786440 | tf_op jit(solution)/shard_map/while/body/eval_jaxpr/ppermute | solution.py:13
  64.7 9.4 %collective-permute-start = (f32[4,128,128]{2,1,0:T(8,128)S(1)}, f32[4,128,128]{2,1,0:T(8,128)S(1)}, u32[]{:S(2)}, u32[]{:S(2)}) collective-permute-start(f32[4,128,128]{2,1,0:T(8,128)S(1)} %multiply_add_fusion.5), channel_id=1, source_target_pairs={{0,8},{8,16},{16,24},{24,32},{32,40},{40,48},{48,56},{56,64},{64,7... | collective-permute-start | bytes 786440 | tf_op jit(solution)/shard_map/while/body/eval_jaxpr/ppermute | solution.py:13
  74.2 9.2 %collective-permute-start = (f32[4,128,128]{2,1,0:T(8,128)S(1)}, f32[4,128,128]{2,1,0:T(8,128)S(1)}, u32[]{:S(2)}, u32[]{:S(2)}) collective-permute-start(f32[4,128,128]{2,1,0:T(8,128)S(1)} %multiply_add_fusion.5), channel_id=1, source_target_pairs={{0,8},{8,16},{16,24},{24,32},{32,40},{40,48},{48,56},{56,64},{64,7... | collective-permute-start | bytes 786440 | tf_op jit(solution)/shard_map/while/body/eval_jaxpr/ppermute | solution.py:13
  83.5 9.3 %collective-permute-start = (f32[4,128,128]{2,1,0:T(8,128)S(1)}, f32[4,128,128]{2,1,0:T(8,128)S(1)}, u32[]{:S(2)}, u32[]{:S(2)}) collective-permute-start(f32[4,128,128]{2,1,0:T(8,128)S(1)} %multiply_add_fusion.5), channel_id=1, source_target_pairs={{0,8},{8,16},{16,24},{24,32},{32,40},{40,48},{48,56},{56,64},{64,7... | collective-permute-start | bytes 786440 | tf_op jit(solution)/shard_map/while/body/eval_jaxpr/ppermute | solution.py:13
  92.8 10.7 %collective-permute-start = (f32[4,128,128]{2,1,0:T(8,128)S(1)}, f32[4,128,128]{2,1,0:T(8,128)S(1)}, u32[]{:S(2)}, u32[]{:S(2)}) collective-permute-start(f32[4,128,128]{2,1,0:T(8,128)S(1)} %multiply_add_fusion.5), channel_id=1, source_target_pairs={{0,8},{8,16},{16,24},{24,32},{32,40},{40,48},{48,56},{56,64},{64,7... | collective-permute-start | bytes 786440 | tf_op jit(solution)/shard_map/while/body/eval_jaxpr/ppermute | solution.py:13
  103.6 12.1 %collective-permute-start = (f32[4,128,128]{2,1,0:T(8,128)S(1)}, f32[4,128,128]{2,1,0:T(8,128)S(1)}, u32[]{:S(2)}, u32[]{:S(2)}) collective-permute-start(f32[4,128,128]{2,1,0:T(8,128)S(1)} %multiply_add_fusion.5), channel_id=1, source_target_pairs={{0,8},{8,16},{16,24},{24,32},{32,40},{40,48},{48,56},{56,64},{64,7... | collective-permute-start | bytes 786440 | tf_op jit(solution)/shard_map/while/body/eval_jaxpr/ppermute | solution.py:13
  115.9 12.3 %collective-permute-start = (f32[4,128,128]{2,1,0:T(8,128)S(1)}, f32[4,128,128]{2,1,0:T(8,128)S(1)}, u32[]{:S(2)}, u32[]{:S(2)}) collective-permute-start(f32[4,128,128]{2,1,0:T(8,128)S(1)} %multiply_add_fusion.5), channel_id=1, source_target_pairs={{0,8},{8,16},{16,24},{24,32},{32,40},{40,48},{48,56},{56,64},{64,7... | collective-permute-start | bytes 786440 | tf_op jit(solution)/shard_map/while/body/eval_jaxpr/ppermute | solution.py:13
  128.2 10.3 %collective-permute-start = (f32[4,128,128]{2,1,0:T(8,128)S(1)}, f32[4,128,128]{2,1,0:T(8,128)S(1)}, u32[]{:S(2)}, u32[]{:S(2)}) collective-permute-start(f32[4,128,128]{2,1,0:T(8,128)S(1)} %multiply_add_fusion.5), channel_id=1, source_target_pairs={{0,8},{8,16},{16,24},{24,32},{32,40},{40,48},{48,56},{56,64},{64,7... | collective-permute-start | bytes 786440 | tf_op jit(solution)/shard_map/while/body/eval_jaxpr/ppermute | solution.py:13
  138.6 8.3 %collective-permute-start = (f32[4,128,128]{2,1,0:T(8,128)S(1)}, f32[4,128,128]{2,1,0:T(8,128)S(1)}, u32[]{:S(2)}, u32[]{:S(2)}) collective-permute-start(f32[4,128,128]{2,1,0:T(8,128)S(1)} %multiply_add_fusion.5), channel_id=1, source_target_pairs={{0,8},{8,16},{16,24},{24,32},{32,40},{40,48},{48,56},{56,64},{64,7... | collective-permute-start | bytes 786440 | tf_op jit(solution)/shard_map/while/body/eval_jaxpr/ppermute | solution.py:13
  147.1 9.5 %collective-permute-start = (f32[4,128,128]{2,1,0:T(8,128)S(1)}, f32[4,128,128]{2,1,0:T(8,128)S(1)}, u32[]{:S(2)}, u32[]{:S(2)}) collective-permute-start(f32[4,128,128]{2,1,0:T(8,128)S(1)} %multiply_add_fusion.5), channel_id=1, source_target_pairs={{0,8},{8,16},{16,24},{24,32},{32,40},{40,48},{48,56},{56,64},{64,7... | collective-permute-start | bytes 786440 | tf_op jit(solution)/shard_map/while/body/eval_jaxpr/ppermute | solution.py:13
  156.7 9.5 %collective-permute-start = (f32[4,128,128]{2,1,0:T(8,128)S(1)}, f32[4,128,128]{2,1,0:T(8,128)S(1)}, u32[]{:S(2)}, u32[]{:S(2)}) collective-permute-start(f32[4,128,128]{2,1,0:T(8,128)S(1)} %multiply_add_fusion.5), channel_id=1, source_target_pairs={{0,8},{8,16},{16,24},{24,32},{32,40},{40,48},{48,56},{56,64},{64,7... | collective-permute-start | bytes 786440 | tf_op jit(solution)/shard_map/while/body/eval_jaxpr/ppermute | solution.py:13
  166.3 9.5 %collective-permute-start = (f32[4,128,128]{2,1,0:T(8,128)S(1)}, f32[4,128,128]{2,1,0:T(8,128)S(1)}, u32[]{:S(2)}, u32[]{:S(2)}) collective-permute-start(f32[4,128,128]{2,1,0:T(8,128)S(1)} %multiply_add_fusion.5), channel_id=1, source_target_pairs={{0,8},{8,16},{16,24},{24,32},{32,40},{40,48},{48,56},{56,64},{64,7... | collective-permute-start | bytes 786440 | tf_op jit(solution)/shard_map/while/body/eval_jaxpr/ppermute | solution.py:13
  175.9 9.2 %collective-permute-start = (f32[4,128,128]{2,1,0:T(8,128)S(1)}, f32[4,128,128]{2,1,0:T(8,128)S(1)}, u32[]{:S(2)}, u32[]{:S(2)}) collective-permute-start(f32[4,128,128]{2,1,0:T(8,128)S(1)} %multiply_add_fusion.5), channel_id=1, source_target_pairs={{0,8},{8,16},{16,24},{24,32},{32,40},{40,48},{48,56},{56,64},{64,7... | collective-permute-start | bytes 786440 | tf_op jit(solution)/shard_map/while/body/eval_jaxpr/ppermute | solution.py:13
  185.2 9.4 %collective-permute-start = (f32[4,128,128]{2,1,0:T(8,128)S(1)}, f32[4,128,128]{2,1,0:T(8,128)S(1)}, u32[]{:S(2)}, u32[]{:S(2)}) collective-permute-start(f32[4,128,128]{2,1,0:T(8,128)S(1)} %multiply_add_fusion.5), channel_id=1, source_target_pairs={{0,8},{8,16},{16,24},{24,32},{32,40},{40,48},{48,56},{56,64},{64,7... | collective-permute-start | bytes 786440 | tf_op jit(solution)/shard_map/while/body/eval_jaxpr/ppermute | solution.py:13
  194.7 10.8 %collective-permute-start = (f32[4,128,128]{2,1,0:T(8,128)S(1)}, f32[4,128,128]{2,1,0:T(8,128)S(1)}, u32[]{:S(2)}, u32[]{:S(2)}) collective-permute-start(f32[4,128,128]{2,1,0:T(8,128)S(1)} %multiply_add_fusion.5), channel_id=1, source_target_pairs={{0,8},{8,16},{16,24},{24,32},{32,40},{40,48},{48,56},{56,64},{64,7... | collective-permute-start | bytes 786440 | tf_op jit(solution)/shard_map/while/body/eval_jaxpr/ppermute | solution.py:13
  205.6 12.3 %collective-permute-start = (f32[4,128,128]{2,1,0:T(8,128)S(1)}, f32[4,128,128]{2,1,0:T(8,128)S(1)}, u32[]{:S(2)}, u32[]{:S(2)}) collective-permute-start(f32[4,128,128]{2,1,0:T(8,128)S(1)} %multiply_add_fusion.5), channel_id=1, source_target_pairs={{0,8},{8,16},{16,24},{24,32},{32,40},{40,48},{48,56},{56,64},{64,7... | collective-permute-start | bytes 786440 | tf_op jit(solution)/shard_map/while/body/eval_jaxpr/ppermute | solution.py:13
  218.0 12.2 %collective-permute-start = (f32[4,128,128]{2,1,0:T(8,128)S(1)}, f32[4,128,128]{2,1,0:T(8,128)S(1)}, u32[]{:S(2)}, u32[]{:S(2)}) collective-permute-start(f32[4,128,128]{2,1,0:T(8,128)S(1)} %multiply_add_fusion.5), channel_id=1, source_target_pairs={{0,8},{8,16},{16,24},{24,32},{32,40},{40,48},{48,56},{56,64},{64,7... | collective-permute-start | bytes 786440 | tf_op jit(solution)/shard_map/while/body/eval_jaxpr/ppermute | solution.py:13
  230.3 9.8 %collective-permute-start = (f32[4,128,128]{2,1,0:T(8,128)S(1)}, f32[4,128,128]{2,1,0:T(8,128)S(1)}, u32[]{:S(2)}, u32[]{:S(2)}) collective-permute-start(f32[4,128,128]{2,1,0:T(8,128)S(1)} %multiply_add_fusion.5), channel_id=1, source_target_pairs={{0,8},{8,16},{16,24},{24,32},{32,40},{40,48},{48,56},{56,64},{64,7... | collective-permute-start | bytes 786440 | tf_op jit(solution)/shard_map/while/body/eval_jaxpr/ppermute | solution.py:13
  240.2 8.3 %collective-permute-start = (f32[4,128,128]{2,1,0:T(8,128)S(1)}, f32[4,128,128]{2,1,0:T(8,128)S(1)}, u32[]{:S(2)}, u32[]{:S(2)}) collective-permute-start(f32[4,128,128]{2,1,0:T(8,128)S(1)} %multiply_add_fusion.5), channel_id=1, source_target_pairs={{0,8},{8,16},{16,24},{24,32},{32,40},{40,48},{48,56},{56,64},{64,7... | collective-permute-start | bytes 786440 | tf_op jit(solution)/shard_map/while/body/eval_jaxpr/ppermute | solution.py:13
  248.6 9.5 %collective-permute-start = (f32[4,128,128]{2,1,0:T(8,128)S(1)}, f32[4,128,128]{2,1,0:T(8,128)S(1)}, u32[]{:S(2)}, u32[]{:S(2)}) collective-permute-start(f32[4,128,128]{2,1,0:T(8,128)S(1)} %multiply_add_fusion.5), channel_id=1, source_target_pairs={{0,8},{8,16},{16,24},{24,32},{32,40},{40,48},{48,56},{56,64},{64,7... | collective-permute-start | bytes 786440 | tf_op jit(solution)/shard_map/while/body/eval_jaxpr/ppermute | solution.py:13
  258.3 9.5 %collective-permute-start = (f32[4,128,128]{2,1,0:T(8,128)S(1)}, f32[4,128,128]{2,1,0:T(8,128)S(1)}, u32[]{:S(2)}, u32[]{:S(2)}) collective-permute-start(f32[4,128,128]{2,1,0:T(8,128)S(1)} %multiply_add_fusion.5), channel_id=1, source_target_pairs={{0,8},{8,16},{16,24},{24,32},{32,40},{40,48},{48,56},{56,64},{64,7... | collective-permute-start | bytes 786440 | tf_op jit(solution)/shard_map/while/body/eval_jaxpr/ppermute | solution.py:13
  267.9 9.5 %collective-permute-start = (f32[4,128,128]{2,1,0:T(8,128)S(1)}, f32[4,128,128]{2,1,0:T(8,128)S(1)}, u32[]{:S(2)}, u32[]{:S(2)}) collective-permute-start(f32[4,128,128]{2,1,0:T(8,128)S(1)} %multiply_add_fusion.5), channel_id=1, source_target_pairs={{0,8},{8,16},{16,24},{24,32},{32,40},{40,48},{48,56},{56,64},{64,7... | collective-permute-start | bytes 786440 | tf_op jit(solution)/shard_map/while/body/eval_jaxpr/ppermute | solution.py:13
  277.5 9.2 %collective-permute-start = (f32[4,128,128]{2,1,0:T(8,128)S(1)}, f32[4,128,128]{2,1,0:T(8,128)S(1)}, u32[]{:S(2)}, u32[]{:S(2)}) collective-permute-start(f32[4,128,128]{2,1,0:T(8,128)S(1)} %multiply_add_fusion.5), channel_id=1, source_target_pairs={{0,8},{8,16},{16,24},{24,32},{32,40},{40,48},{48,56},{56,64},{64,7... | collective-permute-start | bytes 786440 | tf_op jit(solution)/shard_map/while/body/eval_jaxpr/ppermute | solution.py:13
  286.8 9.5 %collective-permute-start = (f32[4,128,128]{2,1,0:T(8,128)S(1)}, f32[4,128,128]{2,1,0:T(8,128)S(1)}, u32[]{:S(2)}, u32[]{:S(2)}) collective-permute-start(f32[4,128,128]{2,1,0:T(8,128)S(1)} %multiply_add_fusion.5), channel_id=1, source_target_pairs={{0,8},{8,16},{16,24},{24,32},{32,40},{40,48},{48,56},{56,64},{64,7... | collective-permute-start | bytes 786440 | tf_op jit(solution)/shard_map/while/body/eval_jaxpr/ppermute | solution.py:13
  296.4 11.0 %collective-permute-start = (f32[4,128,128]{2,1,0:T(8,128)S(1)}, f32[4,128,128]{2,1,0:T(8,128)S(1)}, u32[]{:S(2)}, u32[]{:S(2)}) collective-permute-start(f32[4,128,128]{2,1,0:T(8,128)S(1)} %multiply_add_fusion.5), channel_id=1, source_target_pairs={{0,8},{8,16},{16,24},{24,32},{32,40},{40,48},{48,56},{56,64},{64,7... | collective-permute-start | bytes 786440 | tf_op jit(solution)/shard_map/while/body/eval_jaxpr/ppermute | solution.py:13
  307.5 12.3 %collective-permute-start = (f32[4,128,128]{2,1,0:T(8,128)S(1)}, f32[4,128,128]{2,1,0:T(8,128)S(1)}, u32[]{:S(2)}, u32[]{:S(2)}) collective-permute-start(f32[4,128,128]{2,1,0:T(8,128)S(1)} %multiply_add_fusion.5), channel_id=1, source_target_pairs={{0,8},{8,16},{16,24},{24,32},{32,40},{40,48},{48,56},{56,64},{64,7... | collective-permute-start | bytes 786440 | tf_op jit(solution)/shard_map/while/body/eval_jaxpr/ppermute | solution.py:13
  319.9 11.9 %collective-permute-start = (f32[4,128,128]{2,1,0:T(8,128)S(1)}, f32[4,128,128]{2,1,0:T(8,128)S(1)}, u32[]{:S(2)}, u32[]{:S(2)}) collective-permute-start(f32[4,128,128]{2,1,0:T(8,128)S(1)} %multiply_add_fusion.5), channel_id=1, source_target_pairs={{0,8},{8,16},{16,24},{24,32},{32,40},{40,48},{48,56},{56,64},{64,7... | collective-permute-start | bytes 786440 | tf_op jit(solution)/shard_map/while/body/eval_jaxpr/ppermute | solution.py:13
  338.7 1.6 copy-start.1
Sparse Core Ops, SparseCore 0:
  353.3 169.5 reduce-scatter.1
where the time goes:
time: 534 us; the launch traced here: 532 us
  waiting for transfers between devices  294 us (55%)
  starting transfers between devices  179 us (34%)
  matrix products  23.3 us (4%)
  between operations  13.5 us (3%)
  other arithmetic  12 us (2%)
  local copies, waits for them, and re-layouts  10.1 us (2%)
    ppermute x31, starting transfers between devices, passed_along(): return lax.ppermute(block, axis, route)  179 us
    reduce_scatter x1, waiting for transfers between devices, per_device(): lax.psum_scatter(jnp.dot(hidden, out_weight, preferred_element_type=jnp.f...  170 us
    ppermute x31, waiting for transfers between devices, passed_along(): return lax.ppermute(block, axis, route)  124 us
    dot_general x1, matrix products, per_device(): jnp.dot(hidden, out_weight, preferred_element_type=jnp.float32)  12.9 us
  transfers between devices with their start and end apart: 32, of which 32 were waited for; matrix products, arithmetic and copies ran while one was open for 0% of the time, Pallas kernels for 0%

commit v1 on v0

v1 whole, which is shorter than its diff:
```python
import functools

import jax
import jax.numpy as jnp
from jax import lax
from jax.experimental import pallas as pl
from jax.experimental.pallas import tpu as pltpu
from jax.sharding import PartitionSpec as P

HEAD_DIM = 128
BLOCK = 256
HALF = 128
HEADS = 4
BLOCKS = 4
FEATURES = HEADS * HEAD_DIM
WIDTH = 4096
CHUNK = 512
CHUNKS = WIDTH // CHUNK
SIDE = CHUNKS // 2
WIDE = 1024
PARTS = WIDTH // WIDE
F32 = jnp.float32
BF16 = jnp.bfloat16
MESH = pl.DeviceIdType.MESH
NT = (((1,), (1,)), ((), ()))
TN = (((0,), (0,)), ((), ()))


def head_columns(h):
    return slice(h * HEAD_DIM, (h + 1) * HEAD_DIM)


def kernel(
    seq_size, rate_hbm, k_hbm, v_hbm, q_hbm, g_hbm, w_hbm, out_ref,
    rate, k, v, q, g, w, w_send, w_recv, w_pair,
    run_col, run_row, start, lead, state_send, state_recv, scan_send, scan_recv,
    att, hid, hid_recv, far, plus, minus, own, far_recv, direct_recv, sum_recv,
    load_sem, a_send, a_recv, b_send, b_recv, w_ssem, w_rsem, h_ssem, h_rsem,
    y_send, y_recv,
):
    me = lax.axis_index("seq")
    head = lax.axis_index("head")
    row = head // 2
    core = lax.rem(head, 2)
    partner = row * 2 + (1 - core)
    up = lax.rem(row + 1, 4) * 2 + core
    down = lax.rem(row + 3, 4) * 2 + core
    slice_rows = FEATURES // seq_size
    per_head = HEAD_DIM // slice_rows

    loads = [
        pltpu.make_async_copy(src, dst, load_sem.at[i])
        for i, (src, dst) in enumerate(
            ((rate_hbm, rate), (k_hbm, k), (v_hbm, v), (q_hbm, q), (w_hbm, w), (g_hbm, g))
        )
    ]
    for load in loads:
        load.start()

    barrier = pltpu.get_barrier_semaphore()

    def greet(d, carry):
        peer = lax.rem(me + d, seq_size)
        pl.semaphore_signal(barrier, inc=1, device_id=(peer, head), device_id_type=MESH)
        return carry

    lax.fori_loop(1, seq_size, greet, 0)
    for other in (partner, up, down):
        pl.semaphore_signal(barrier, inc=1, device_id=(me, other), device_id_type=MESH)

    low = lax.broadcasted_iota(jnp.int32, (BLOCK, BLOCK), 0)
    high = lax.broadcasted_iota(jnp.int32, (BLOCK, BLOCK), 1)
    upper = jnp.where(low <= high, 1.0, 0.0).astype(F32)
    lower = jnp.where(low >= high, 1.0, 0.0).astype(F32)
    loads[0].wait()
    for b in range(BLOCKS):
        rates = rate[:, b * BLOCK:(b + 1) * BLOCK]
        run_row[b] = jnp.dot(
            rates, upper, preferred_element_type=F32, precision=lax.Precision.HIGHEST
        )
        run_col[b] = lax.dot_general(
            lower, rates, NT, preferred_element_type=F32, precision=lax.Precision.HIGHEST
        )
    loads[1].wait()
    loads[2].wait()
    for h in range(HEADS):
        state = jnp.zeros((HEAD_DIM, HEAD_DIM), F32)
        ahead = jnp.zeros((1, 1), F32)
        for b in range(BLOCKS):
            rows = slice(b * BLOCK, (b + 1) * BLOCK)
            run = run_col[b, :, h:h + 1]
            total = run[BLOCK - 1:BLOCK, :]
            start[b, h] = state
            lead[b, h] = jnp.broadcast_to(jnp.exp(ahead), (8, HEAD_DIM))
            keys = (k[rows, head_columns(h)].astype(F32) * jnp.exp(total - run)).astype(BF16)
            added = lax.dot_general(
                keys, v[rows, head_columns(h)], TN, preferred_element_type=F32
            )
            state = jnp.exp(total) * state + added
            ahead = ahead + total
        through = jnp.broadcast_to(jnp.exp(ahead), (per_head, 8, HEAD_DIM))
        pieces = pl.ds(h * per_head, per_head)
        state_send[pieces, 0:slice_rows, :] = state.reshape(per_head, slice_rows, HEAD_DIM)
        state_send[pieces, slice_rows:slice_rows + 8, :] = through

    pl.semaphore_wait(barrier, seq_size + 2)

    def slice_out(peer):
        return pltpu.make_async_remote_copy(
            src_ref=state_send.at[peer], dst_ref=state_recv.at[me],
            send_sem=a_send.at[peer], recv_sem=a_recv.at[me],
            device_id=(peer, head), device_id_type=MESH,
        )

    def slice_in(peer):
        return pltpu.make_async_remote_copy(
            src_ref=state_send.at[peer], dst_ref=state_recv.at[peer],
            send_sem=a_send.at[peer], recv_sem=a_recv.at[peer],
            device_id=(peer, head), device_id_type=MESH,
        )

    def scan_out(peer):
        return pltpu.make_async_remote_copy(
            src_ref=scan_send.at[peer], dst_ref=scan_recv.at[me],
            send_sem=b_send.at[peer], recv_sem=b_recv.at[me],
            device_id=(peer, head), device_id_type=MESH,
        )

    def scan_in(peer):
        return pltpu.make_async_remote_copy(
            src_ref=scan_send.at[peer], dst_ref=scan_recv.at[peer],
            send_sem=b_send.at[peer], recv_sem=b_recv.at[peer],
            device_id=(peer, head), device_id_type=MESH,
        )

    def send_slice(d, carry):
        slice_out(lax.rem(me + d, seq_size)).start()
        return carry

    lax.fori_loop(1, seq_size, send_slice, 0)
    state_recv[me] = state_send[me]

    loads[4].wait()
    pair_copies = []
    for i in range(PARTS):
        columns = slice(i * WIDE, (i + 1) * WIDE)
        w_send[i] = w[:, columns].astype(F32)
        pair_copies.append(
            pltpu.make_async_remote_copy(
                src_ref=w_send.at[i], dst_ref=w_recv.at[i],
                send_sem=w_ssem.at[i], recv_sem=w_rsem.at[i],
                device_id=(me, partner), device_id_type=MESH,
            )
        )
        pair_copies[-1].start()

    loads[3].wait()
    causal = low >= high

    def inside(b, carry):
        rows = pl.ds(pl.multiple_of(b * BLOCK, BLOCK), BLOCK)
        for h in range(HEADS):
            scores = lax.dot_general(
                q[rows, head_columns(h)], k[rows, head_columns(h)], NT,
                preferred_element_type=F32,
            )
            spread = run_col[b, :, h:h + 1] - run_row[b, h:h + 1, :]
            decay = jnp.exp(jnp.where(causal, spread, -1e30))
            weights = (scores * decay).astype(BF16)
            att[rows, head_columns(h)] = jnp.dot(
                weights, v[rows, head_columns(h)], preferred_element_type=F32
            )
        return carry

    lax.fori_loop(0, BLOCKS - 1, inside, 0)

    def arrive(d, carry):
        slice_in(lax.rem(me + d, seq_size)).wait_recv()
        return carry

    lax.fori_loop(1, seq_size, arrive, 0)

    def scan(p, state):
        scan_send[p] = state
        return state_recv[p, slice_rows:slice_rows + 1, :] * state + state_recv[p, 0:slice_rows, :]

    lax.fori_loop(0, seq_size, scan, jnp.zeros((slice_rows, HEAD_DIM), F32))

    def send_scan(d, carry):
        scan_out(lax.rem(me + d, seq_size)).start()
        return carry

    lax.fori_loop(1, seq_size, send_scan, 0)
    scan_recv[me] = scan_send[me]

    inside(BLOCKS - 1, 0)
    loads[5].wait()
    for i in range(PARTS):
        pair_copies[i].wait_recv()
        w_pair[:, i * WIDE:(i + 1) * WIDE] = w_recv[i].astype(BF16)

    def arrive_scan(d, carry):
        scan_in(lax.rem(me + d, seq_size)).wait_recv()
        return carry

    lax.fori_loop(1, seq_size, arrive_scan, 0)

    hid_copies = []

    def hide(t, b):
        rows = pl.ds(pl.multiple_of(b * BLOCK, BLOCK), BLOCK)
        for h in range(HEADS):
            incoming = scan_recv[h * per_head:(h + 1) * per_head].reshape(HEAD_DIM, HEAD_DIM)
            state = start[b, h] + lead[b, h, 0:1, :] * incoming
            top = state.astype(BF16)
            rest = (state - top.astype(F32)).astype(BF16)
            queries = q[rows, head_columns(h)]
            carried = jnp.dot(queries, top, preferred_element_type=F32) + jnp.dot(
                queries, rest, preferred_element_type=F32
            )
            attended = att[rows, head_columns(h)] + carried * jnp.exp(run_col[b, :, h:h + 1])
            mean = jnp.mean(attended * attended, axis=-1, keepdims=True)
            gate = g[rows, head_columns(h)].astype(F32)
            gated = attended * lax.rsqrt(mean + 1e-6) * (gate / (1.0 + jnp.exp(-gate)))
            hid[t, :, :, head_columns(h)] = gated.astype(BF16).astype(F32).reshape(
                2, HALF, HEAD_DIM
            )
        copy = pltpu.make_async_remote_copy(
            src_ref=hid.at[t, 1 - core], dst_ref=hid_recv.at[t],
            send_sem=h_ssem.at[t], recv_sem=h_rsem.at[t],
            device_id=(me, partner), device_id_type=MESH,
        )
        copy.start()
        hid_copies.append(copy)

    def project(t, n):
        columns = slice(n * CHUNK, (n + 1) * CHUNK)
        return jnp.dot(
            hid[t, core].astype(BF16), w[:, columns], preferred_element_type=F32
        ) + jnp.dot(hid_recv[t].astype(BF16), w_pair[:, columns], preferred_element_type=F32)

    def across(kind, n, src, dst, other):
        return pltpu.make_async_remote_copy(
            src_ref=src, dst_ref=dst, send_sem=y_send.at[kind, n], recv_sem=y_recv.at[kind, n],
            device_id=(me, other), device_id_type=MESH,
        )

    blocks = [lax.rem(row + 2, 4), lax.rem(row + 1, 4), lax.rem(row + 3, 4), row]
    far_copies = [
        across(0, n, far.at[n], far_recv.at[n], up if n < SIDE else down) for n in range(CHUNKS)
    ]
    direct_copies = [
        across(
            1, n, minus.at[n] if n < SIDE else plus.at[n], direct_recv.at[n],
            down if n < SIDE else up,
        )
        for n in range(CHUNKS)
    ]
    sum_copies = [
        across(
            2, n, plus.at[n] if n < SIDE else minus.at[n], sum_recv.at[n],
            up if n < SIDE else down,
        )
        for n in range(CHUNKS)
    ]
    order = [n // 2 + (n % 2) * SIDE for n in range(CHUNKS)]

    hide(0, blocks[0])
    hide(1, blocks[1])
    hid_copies[0].wait_recv()
    for n in order:
        far[n] = project(0, n)
        far_copies[n].start()
    hide(2, blocks[2])
    hid_copies[1].wait_recv()
    for n in range(SIDE, CHUNKS):
        plus[n] = project(1, n)
        direct_copies[n].start()
    hid_copies[2].wait_recv()
    for n in range(SIDE):
        minus[n] = project(2, n)
        direct_copies[n].start()
    for n in range(SIDE):
        plus[n] = project(1, n)
        minus[SIDE + n] = project(2, SIDE + n)
        far_copies[n].wait_recv()
        plus[n] += far_recv[n]
        sum_copies[n].start()
        far_copies[SIDE + n].wait_recv()
        minus[SIDE + n] += far_recv[SIDE + n]
        sum_copies[SIDE + n].start()
    hide(3, blocks[3])
    hid_copies[3].wait_recv()
    for n in order:
        own[n] = project(3, n)
    for n in order:
        direct_copies[n].wait_recv()
        own[n] += direct_recv[n]
    for n in order:
        sum_copies[n].wait_recv()
        out_ref[:, n * CHUNK:(n + 1) * CHUNK] = (own[n] + sum_recv[n]).astype(BF16)

    def settle(d, carry):
        peer = lax.rem(me + d, seq_size)
        slice_out(peer).wait_send()
        scan_out(peer).wait_send()
        return carry

    lax.fori_loop(1, seq_size, settle, 0)
    for copy in pair_copies + hid_copies + far_copies + direct_copies + sum_copies:
        copy.wait_send()


def per_device(seq_size, queries, key_vectors, value_vectors, gate_input, log_decay, out_weight):
    tokens = BLOCKS * BLOCK
    slice_rows = FEATURES // seq_size
    whole = pl.BlockSpec(memory_space=pl.ANY)
    dma = pltpu.SemaphoreType.DMA
    vmem = pltpu.VMEM
    return pl.pallas_call(
        functools.partial(kernel, seq_size),
        out_shape=jax.ShapeDtypeStruct((HALF, WIDTH), BF16),
        in_specs=[whole] * 6,
        out_specs=pl.BlockSpec(memory_space=pltpu.VMEM),
        scratch_shapes=[
            vmem((HEADS, tokens), F32),
            vmem((tokens, FEATURES), BF16),
            vmem((tokens, FEATURES), BF16),
            vmem((tokens, FEATURES), BF16),
            vmem((tokens, FEATURES), BF16),
            vmem((FEATURES, WIDTH), BF16),
            vmem((PARTS, FEATURES, WIDE), F32),
            vmem((PARTS, FEATURES, WIDE), F32),
            vmem((FEATURES, WIDTH), BF16),
            vmem((BLOCKS, BLOCK, HEADS), F32),
            vmem((BLOCKS, HEADS, BLOCK), F32),
            vmem((BLOCKS, HEADS, HEAD_DIM, HEAD_DIM), F32),
            vmem((BLOCKS, HEADS, 8, HEAD_DIM), F32),
            vmem((seq_size, slice_rows + 8, HEAD_DIM), F32),
            vmem((seq_size, slice_rows + 8, HEAD_DIM), F32),
            vmem((seq_size, slice_rows, HEAD_DIM), F32),
            vmem((seq_size, slice_rows, HEAD_DIM), F32),
            vmem((tokens, FEATURES), F32),
            vmem((BLOCKS, 2, HALF, FEATURES), F32),
            vmem((BLOCKS, HALF, FEATURES), F32),
            vmem((CHUNKS, HALF, CHUNK), F32),
            vmem((CHUNKS, HALF, CHUNK), F32),
            vmem((CHUNKS, HALF, CHUNK), F32),
            vmem((CHUNKS, HALF, CHUNK), F32),
            vmem((CHUNKS, HALF, CHUNK), F32),
            vmem((CHUNKS, HALF, CHUNK), F32),
            vmem((CHUNKS, HALF, CHUNK), F32),
            dma((6,)),
            dma((seq_size,)), dma((seq_size,)), dma((seq_size,)), dma((seq_size,)),
            dma((PARTS,)), dma((PARTS,)), dma((BLOCKS,)), dma((BLOCKS,)),
            dma((3, CHUNKS)), dma((3, CHUNKS)),
        ],
        compiler_params=pltpu.CompilerParams(
            collective_id=0, has_side_effects=True, vmem_limit_bytes=62 * 1024 * 1024
        ),
    )(log_decay.T, key_vectors, value_vectors, queries, gate_input, out_weight)


def solution(mesh):
    placed = (
        P("seq", "head"),
        P("seq", "head"),
        P("seq", "head"),
        P("seq", "head"),
        P("seq", "head"),
        P("head", None),
    )
    return jax.shard_map(
        functools.partial(per_device, mesh.shape["seq"]),
        mesh=mesh, in_specs=placed, out_specs=P(("seq", "head"), None), check_vma=False,
    )
```

time: 534 us -> 110 us (0.21)
  waiting for transfers between devices: 294 us -> 0 us
  starting transfers between devices: 179 us -> 0 us
  Pallas kernels: 0 us -> 108 us
  matrix products: 23.3 us -> 0 us
  between operations: 13.5 us -> 0.01 us
  other arithmetic: 12 us -> 0 us
  local copies, waits for them, and re-layouts: 10.1 us -> 2.29 us
    ppermute x31 -> x0, starting transfers between devices: 179 us -> none  [passed_along(): return lax.ppermute(block, axis, route)]
    reduce_scatter x1 -> x0, waiting for transfers between devices: 170 us -> none  [per_device(): lax.psum_scatter(jnp.dot(hidden, out_weight, preferred_element_type=jnp.f...]
    ppermute x31 -> x0, waiting for transfers between devices: 124 us -> none  [passed_along(): return lax.ppermute(block, axis, route)]
    pallas_call x0 -> x1, Pallas kernels: none -> 108 us  [per_device(): pl.pallas_call(functools.partial(kernel, seq_size), out_shape=jax.ShapeDt...]
    dot_general x4 -> x0, matrix products: 23.3 us -> none  [the longest x1 12.9 us: per_device(): jnp.dot(hidden, out_weight, preferred_element_type=jnp.float32)]
    reshape x7 -> x0, local copies, waits for them, and re-layouts: 6 us -> none  [the longest x2 2.65 us: per_device(): key_blocks = key_vectors.reshape(split_shape)]
  transfers between devices with their start and end apart: 32 -> 0, of which waited for: 32 -> 0; matrix products, arithmetic and copies ran while one was open for 0% -> 0% of each run, Pallas kernels for 0% -> 0%
where the time goes in v1:
time: 110 us
  Pallas kernels  108 us (98%)
  local copies, waits for them, and re-layouts  2.29 us (2%)
    pallas_call x1, Pallas kernels, per_device(): pl.pallas_call(functools.partial(kernel, seq_size), out_shape=jax.ShapeDt...  108 us
    unnamed x1, local copies, waits for them, and re-layouts  2.29 us

profile of v1, /device:TPU:1, one launch (start us, length us, event | category | flops | bytes accessed | tf_op | source)
XLA Modules:
  0.0 109.8 jit_solution(9219829373864738990)
XLA Ops:
  0.0 107.5 %shard_map.64 = bf16[128,4096]{1,0:T(8,128)(2,1)} custom-call(f32[4,1024]{1,0:T(4,128)} %bitcast.1, bf16[1024,512]{1,0:T(8,128)(2,1)} %k_hbm.1, bf16[1024,512]{1,0:T(8,128)(2,1)} %v_hbm.1, bf16[1024,512]{1,0:T(8,128)(2,1)} %q_hbm.1, bf16[1024,512]{1,0:T(8,128)(2,1)} %g_hbm.1, bf16[512,4096]{1,0:T(8,128)(2,1)} %w_hbm.1), custom_call_target="tpu_custom_call" | custom-call | tf_op jit(solution)/shard_map/pallas_call | solution.py:320
  107.5 2.3 %copy.8 = bf16[128,4096]{1,0:T(8,128)(2,1)} copy(bf16[128,4096]{1,0:T(8,128)(2,1)} %shard_map.64) | data formatting | bytes 2097152

commit v2 on v1

v2 whole, which is shorter than its diff:
```python
import functools

import jax
import jax.numpy as jnp
from jax import lax
from jax.experimental import pallas as pl
from jax.experimental.pallas import tpu as pltpu
from jax.sharding import PartitionSpec as P

HEAD_DIM = 128
BLOCK = 256
HALF = 128
HEADS = 4
BLOCKS = 4
FEATURES = HEADS * HEAD_DIM
WIDTH = 4096
CHUNK = 512
CHUNKS = WIDTH // CHUNK
SIDE = CHUNKS // 2
F32 = jnp.float32
BF16 = jnp.bfloat16
MESH = pl.DeviceIdType.MESH
NT = (((1,), (1,)), ((), ()))
TN = (((0,), (0,)), ((), ()))


def head_columns(h):
    return slice(h * HEAD_DIM, (h + 1) * HEAD_DIM)


def kernel(
    seq_size, rate_hbm, k_hbm, v_hbm, q_hbm, g_hbm, w_hbm, out_ref,
    rate, padded, k, v, q, g, w, w_send, w_recv, w_pair,
    run_col, run_row, start, lead, state_send, state_recv, scan_send, scan_recv,
    att, since, silu, entry, hid, hid_recv, far, plus, minus, own, far_recv, direct_recv,
    sum_recv, result,
    load_sem, a_send, a_recv, w_ssem, w_rsem, h_ssem, h_rsem,
    y_send, y_recv, o_sem,
):
    me = lax.axis_index("seq")
    head = lax.axis_index("head")
    row = head // 2
    core = lax.rem(head, 2)
    partner = row * 2 + (1 - core)
    up = lax.rem(row + 1, 4) * 2 + core
    down = lax.rem(row + 3, 4) * 2 + core
    slice_rows = FEATURES // seq_size
    per_head = HEAD_DIM // slice_rows

    loads = [
        pltpu.make_async_copy(src, dst, load_sem.at[i])
        for i, (src, dst) in enumerate(
            ((rate_hbm, rate), (k_hbm, k), (v_hbm, v), (q_hbm, q), (w_hbm, w), (g_hbm, g))
        )
    ]
    for load in loads:
        load.start()

    barrier = pltpu.get_barrier_semaphore()

    def greet(d, carry):
        peer = lax.rem(me + d, seq_size)
        pl.semaphore_signal(barrier, inc=1, device_id=(peer, head), device_id_type=MESH)
        return carry

    lax.fori_loop(1, seq_size, greet, 0)
    for other in (partner, up, down):
        pl.semaphore_signal(barrier, inc=1, device_id=(me, other), device_id_type=MESH)

    low = lax.broadcasted_iota(jnp.int32, (BLOCK, BLOCK), 0)
    high = lax.broadcasted_iota(jnp.int32, (BLOCK, BLOCK), 1)
    upper = jnp.where(low <= high, 1.0, 0.0).astype(BF16)
    lower = jnp.where(low >= high, 1.0, 0.0).astype(BF16)
    loads[0].wait()
    for b in range(BLOCKS):
        padded[b, 0:HEADS, :] = rate[:, b * BLOCK:(b + 1) * BLOCK]
        padded[b, HEADS:8, :] = jnp.zeros((8 - HEADS, BLOCK), F32)
    rates = padded[...].reshape(BLOCKS * 8, BLOCK)
    run_rows = jnp.zeros((BLOCKS * 8, BLOCK), F32)
    run_cols = jnp.zeros((BLOCK, BLOCKS * 8), F32)
    for _ in range(3):
        piece = rates.astype(BF16)
        run_rows += jnp.dot(piece, upper, preferred_element_type=F32)
        run_cols += lax.dot_general(lower, piece, NT, preferred_element_type=F32)
        rates = rates - piece.astype(F32)
    run_row[...] = run_rows.reshape(BLOCKS, 8, BLOCK)
    for b in range(BLOCKS):
        run_col[b] = run_cols[:, 8 * b:8 * b + 8]
    totals = run_rows[:, BLOCK - 1:BLOCK]
    key_scale = jnp.exp(totals - run_rows)
    block_decay = jnp.broadcast_to(jnp.exp(totals), (BLOCKS * 8, HEAD_DIM))
    ahead = jnp.zeros((8, 1), F32)
    for b in range(BLOCKS):
        lead[b] = jnp.broadcast_to(jnp.exp(ahead), (8, HEAD_DIM))
        ahead = ahead + totals[8 * b:8 * b + 8]
    through = jnp.broadcast_to(jnp.exp(ahead), (8, HEAD_DIM))
    loads[1].wait()
    loads[2].wait()
    for h in range(HEADS):
        state = jnp.zeros((HEAD_DIM, HEAD_DIM), F32)
        for b in range(BLOCKS):
            rows = slice(b * BLOCK, (b + 1) * BLOCK)
            line = slice(8 * b + h, 8 * b + h + 1)
            start[b, h] = state
            keys = (k[rows, head_columns(h)].T.astype(F32) * key_scale[line]).astype(BF16)
            added = jnp.dot(keys, v[rows, head_columns(h)], preferred_element_type=F32)
            state = block_decay[line] * state + added
        pieces = pl.ds(h * per_head, per_head)
        state_send[pieces, 0:slice_rows, :] = state.reshape(per_head, slice_rows, HEAD_DIM)
        state_send[pieces, slice_rows:slice_rows + 8, :] = jnp.broadcast_to(
            through[h:h + 1], (per_head, 8, HEAD_DIM)
        )

    pl.semaphore_wait(barrier, seq_size + 2)

    def exchange(phase, src, dst, peer):
        return pltpu.make_async_remote_copy(
            src_ref=src, dst_ref=dst, send_sem=a_send.at[phase], recv_sem=a_recv.at[phase],
            device_id=(peer, head), device_id_type=MESH,
        )

    others = pl.ds(0, seq_size - 1)
    next_peer = lax.rem(me + 1, seq_size)
    all_slices = exchange(0, state_send.at[others], state_recv.at[others], next_peer)
    all_scans = exchange(1, scan_send.at[others], scan_recv.at[others], next_peer)

    def send_slice(d, carry):
        peer = lax.rem(me + d, seq_size)
        exchange(0, state_send.at[peer], state_recv.at[me], peer).start()
        return carry

    lax.fori_loop(1, seq_size, send_slice, 0)
    state_recv[me] = state_send[me]

    blocks = [lax.rem(row + 2, 4), lax.rem(row + 1, 4), lax.rem(row + 3, 4), row]
    order = [n // 2 + (n % 2) * SIDE for n in range(CHUNKS)]

    def columns(n):
        return slice(n * CHUNK, (n + 1) * CHUNK)

    loads[4].wait()
    pair_copies = {}
    for n in order:
        w_send[n] = w[:, columns(n)].astype(F32)
        pair_copies[n] = pltpu.make_async_remote_copy(
            src_ref=w_send.at[n], dst_ref=w_recv.at[n],
            send_sem=w_ssem.at[n], recv_sem=w_rsem.at[n],
            device_id=(me, partner), device_id_type=MESH,
        )
        pair_copies[n].start()

    def receive_weights(n):
        pair_copies[n].wait_recv()
        w_pair[:, columns(n)] = w_recv[n].astype(BF16)

    loads[3].wait()
    loads[5].wait()
    causal = low >= high

    def inside(b):
        rows = pl.ds(pl.multiple_of(b * BLOCK, BLOCK), BLOCK)
        for h in range(HEADS):
            scores = lax.dot_general(
                q[rows, head_columns(h)], k[rows, head_columns(h)], NT,
                preferred_element_type=F32,
            )
            run = run_col[b, :, h:h + 1]
            decay = jnp.exp(jnp.where(causal, run - run_row[b, h:h + 1, :], -1e30))
            weights = (scores * decay).astype(BF16)
            att[rows, head_columns(h)] = jnp.dot(
                weights, v[rows, head_columns(h)], preferred_element_type=F32
            )
            since[rows, head_columns(h)] = jnp.broadcast_to(jnp.exp(run), (BLOCK, HEAD_DIM))
            gate = g[rows, head_columns(h)].astype(F32)
            silu[rows, head_columns(h)] = gate / (1.0 + jnp.exp(-gate))

    inside(blocks[0])
    inside(blocks[1])

    all_slices.wait_recv()

    def scan(p, state):
        scan_send[p] = state
        return state_recv[p, slice_rows:slice_rows + 1, :] * state + state_recv[p, 0:slice_rows, :]

    lax.fori_loop(0, seq_size, scan, jnp.zeros((slice_rows, HEAD_DIM), F32), unroll=4)

    def send_scan(d, carry):
        peer = lax.rem(me + d, seq_size)
        exchange(1, scan_send.at[peer], scan_recv.at[me], peer).start()
        return carry

    lax.fori_loop(1, seq_size, send_scan, 0)
    scan_recv[me] = scan_send[me]

    inside(blocks[2])
    inside(blocks[3])
    for n in order[:SIDE]:
        receive_weights(n)
    all_scans.wait_recv()

    hid_copies = []

    def hide(t):
        b = blocks[t]
        for h in range(HEADS):
            incoming = scan_recv[h * per_head:(h + 1) * per_head].reshape(HEAD_DIM, HEAD_DIM)
            state = start[b, h] + lead[b, h:h + 1, :] * incoming
            top = state.astype(BF16)
            entry[0, h] = top
            entry[1, h] = (state - top.astype(F32)).astype(BF16)
        for side in (1 - core, core):
            rows = pl.ds(pl.multiple_of(b * BLOCK + side * HALF, HALF), HALF)
            for h in range(HEADS):
                queries = q[rows, head_columns(h)]
                carried = jnp.dot(queries, entry[0, h], preferred_element_type=F32) + jnp.dot(
                    queries, entry[1, h], preferred_element_type=F32
                )
                attended = att[rows, head_columns(h)] + carried * since[rows, head_columns(h)]
                mean = jnp.mean(attended * attended, axis=-1, keepdims=True)
                gated = attended * lax.rsqrt(mean + 1e-6) * silu[rows, head_columns(h)]
                hid[t, side, :, head_columns(h)] = gated.astype(BF16).astype(F32)
            if side is not core:
                copy = pltpu.make_async_remote_copy(
                    src_ref=hid.at[t, 1 - core], dst_ref=hid_recv.at[t],
                    send_sem=h_ssem.at[t], recv_sem=h_rsem.at[t],
                    device_id=(me, partner), device_id_type=MESH,
                )
                copy.start()
                hid_copies.append(copy)

    def project(t, n):
        return jnp.dot(
            hid[t, core].astype(BF16), w[:, columns(n)], preferred_element_type=F32
        ) + jnp.dot(hid_recv[t].astype(BF16), w_pair[:, columns(n)], preferred_element_type=F32)

    def across(kind, n, src, dst, other):
        return pltpu.make_async_remote_copy(
            src_ref=src, dst_ref=dst, send_sem=y_send.at[kind, n], recv_sem=y_recv.at[kind, n],
            device_id=(me, other), device_id_type=MESH,
        )

    far_copies = [
        across(0, n, far.at[n], far_recv.at[n], up if n < SIDE else down) for n in range(CHUNKS)
    ]
    direct_copies = [
        across(
            1, n, minus.at[n] if n < SIDE else plus.at[n], direct_recv.at[n],
            down if n < SIDE else up,
        )
        for n in range(CHUNKS)
    ]
    sum_copies = [
        across(
            2, n, plus.at[n] if n < SIDE else minus.at[n], sum_recv.at[n],
            up if n < SIDE else down,
        )
        for n in range(CHUNKS)
    ]

    hide(0)
    hid_copies[0].wait_recv()
    for i, n in enumerate(order):
        if i >= SIDE:
            receive_weights(n)
        far[n] = project(0, n)
        far_copies[n].start()
    hide(1)
    hide(2)
    hid_copies[1].wait_recv()
    for n in range(SIDE, CHUNKS):
        plus[n] = project(1, n)
        direct_copies[n].start()
    hid_copies[2].wait_recv()
    for n in range(SIDE):
        minus[n] = project(2, n)
        direct_copies[n].start()
    for n in range(SIDE):
        plus[n] = project(1, n)
        minus[SIDE + n] = project(2, SIDE + n)
        far_copies[n].wait_recv()
        plus[n] += far_recv[n]
        sum_copies[n].start()
        far_copies[SIDE + n].wait_recv()
        minus[SIDE + n] += far_recv[SIDE + n]
        sum_copies[SIDE + n].start()
    hide(3)
    hid_copies[3].wait_recv()
    for n in order:
        own[n] = project(3, n)
    for n in order:
        direct_copies[n].wait_recv()
        own[n] += direct_recv[n]
    out_copies = []
    for n in order:
        sum_copies[n].wait_recv()
        result[:, columns(n)] = (own[n] + sum_recv[n]).astype(BF16)
        out_copies.append(
            pltpu.make_async_copy(
                result.at[:, columns(n)], out_ref.at[:, columns(n)], o_sem.at[n]
            )
        )
        out_copies[-1].start()

    all_slices.wait_send()
    all_scans.wait_send()
    for copy in list(pair_copies.values()) + hid_copies + far_copies + direct_copies + sum_copies:
        copy.wait_send()
    for copy in out_copies:
        copy.wait()


def per_device(seq_size, queries, key_vectors, value_vectors, gate_input, log_decay, out_weight):
    tokens = BLOCKS * BLOCK
    slice_rows = FEATURES // seq_size
    whole = pl.BlockSpec(memory_space=pl.ANY)
    dma = pltpu.SemaphoreType.DMA
    vmem = pltpu.VMEM
    return pl.pallas_call(
        functools.partial(kernel, seq_size),
        out_shape=jax.ShapeDtypeStruct((HALF, WIDTH), BF16),
        in_specs=[whole] * 6,
        out_specs=whole,
        scratch_shapes=[
            vmem((HEADS, tokens), F32),
            vmem((BLOCKS, 8, BLOCK), F32),
            vmem((tokens, FEATURES), BF16),
            vmem((tokens, FEATURES), BF16),
            vmem((tokens, FEATURES), BF16),
            vmem((tokens, FEATURES), BF16),
            vmem((FEATURES, WIDTH), BF16),
            vmem((CHUNKS, FEATURES, CHUNK), F32),
            vmem((CHUNKS, FEATURES, CHUNK), F32),
            vmem((FEATURES, WIDTH), BF16),
            vmem((BLOCKS, BLOCK, 8), F32),
            vmem((BLOCKS, 8, BLOCK), F32),
            vmem((BLOCKS, HEADS, HEAD_DIM, HEAD_DIM), F32),
            vmem((BLOCKS, 8, HEAD_DIM), F32),
            vmem((seq_size, slice_rows + 8, HEAD_DIM), F32),
            vmem((seq_size, slice_rows + 8, HEAD_DIM), F32),
            vmem((seq_size, slice_rows, HEAD_DIM), F32),
            vmem((seq_size, slice_rows, HEAD_DIM), F32),
            vmem((tokens, FEATURES), F32),
            vmem((tokens, FEATURES), F32),
            vmem((tokens, FEATURES), F32),
            vmem((2, HEADS, HEAD_DIM, HEAD_DIM), BF16),
            vmem((BLOCKS, 2, HALF, FEATURES), F32),
            vmem((BLOCKS, HALF, FEATURES), F32),
            vmem((CHUNKS, HALF, CHUNK), F32),
            vmem((CHUNKS, HALF, CHUNK), F32),
            vmem((CHUNKS, HALF, CHUNK), F32),
            vmem((CHUNKS, HALF, CHUNK), F32),
            vmem((CHUNKS, HALF, CHUNK), F32),
            vmem((CHUNKS, HALF, CHUNK), F32),
            vmem((CHUNKS, HALF, CHUNK), F32),
            vmem((HALF, WIDTH), BF16),
            dma((6,)), dma((2,)), dma((2,)), dma((CHUNKS,)), dma((CHUNKS,)), dma((BLOCKS,)), dma((BLOCKS,)),
            dma((3, CHUNKS)), dma((3, CHUNKS)), dma((CHUNKS,)),
        ],
        compiler_params=pltpu.CompilerParams(
            collective_id=0, has_side_effects=True, vmem_limit_bytes=62 * 1024 * 1024
        ),
    )(log_decay.T, key_vectors, value_vectors, queries, gate_input, out_weight)


def solution(mesh):
    placed = (
        P("seq", "head"),
        P("seq", "head"),
        P("seq", "head"),
        P("seq", "head"),
        P("seq", "head"),
        P("head", None),
    )
    return jax.shard_map(
        functools.partial(per_device, mesh.shape["seq"]),
        mesh=mesh, in_specs=placed, out_specs=P(("seq", "head"), None), check_vma=False,
    )
```

time: 110 us -> 108 us (0.982)
  Pallas kernels: 108 us -> 106 us
    pallas_call x1, Pallas kernels: 108 us -> 106 us  [per_device(): pl.pallas_call(functools.partial(kernel, seq_size), out_shape=jax.ShapeDt...]
where the time goes in v2:
time: 108 us
  Pallas kernels  106 us (98%)
  local copies, waits for them, and re-layouts  2.29 us (2%)
    pallas_call x1, Pallas kernels, per_device(): pl.pallas_call(functools.partial(kernel, seq_size), out_shape=jax.ShapeDt...  106 us
    unnamed x1, local copies, waits for them, and re-layouts  2.29 us

profile of v2, /device:TPU:1, one launch (start us, length us, event | category | flops | bytes accessed | tf_op | source)
XLA Modules:
  0.0 108.3 jit_solution(5377251388962238439)
XLA Ops:
  0.0 106.0 %shard_map.64 = bf16[128,4096]{1,0:T(8,128)(2,1)} custom-call(f32[4,1024]{1,0:T(4,128)} %bitcast.1, bf16[1024,512]{1,0:T(8,128)(2,1)} %k_hbm.1, bf16[1024,512]{1,0:T(8,128)(2,1)} %v_hbm.1, bf16[1024,512]{1,0:T(8,128)(2,1)} %q_hbm.1, bf16[1024,512]{1,0:T(8,128)(2,1)} %g_hbm.1, bf16[512,4096]{1,0:T(8,128)(2,1)} %w_hbm.1), custom_call_target="tpu_custom_call" | custom-call | tf_op jit(solution)/shard_map/pallas_call | solution.py:319
  106.0 2.3 %copy.8 = bf16[128,4096]{1,0:T(8,128)(2,1)} copy(bf16[128,4096]{1,0:T(8,128)(2,1)} %shard_map.64) | data formatting | bytes 2097152

commit v3 on v2

--- a/solution.py
+++ b/solution.py
@@ -53,7 +53,7 @@
             ((rate_hbm, rate), (k_hbm, k), (v_hbm, v), (q_hbm, q), (w_hbm, w), (g_hbm, g))
         )
     ]
-    for load in loads:
+    for load in loads[:3]:
         load.start()
 
     barrier = pltpu.get_barrier_semaphore()
@@ -96,6 +96,8 @@
     through = jnp.broadcast_to(jnp.exp(ahead), (8, HEAD_DIM))
     loads[1].wait()
     loads[2].wait()
+    for load in loads[3:]:
+        load.start()
     for h in range(HEADS):
         state = jnp.zeros((HEAD_DIM, HEAD_DIM), F32)
         for b in range(BLOCKS):
@@ -121,15 +123,26 @@
 
     others = pl.ds(0, seq_size - 1)
     next_peer = lax.rem(me + 1, seq_size)
-    all_slices = exchange(0, state_send.at[others], state_recv.at[others], next_peer)
+    message = pl.ds(0, slice_rows + 1)
+    all_slices = exchange(
+        0, state_send.at[others, message], state_recv.at[others, message], next_peer
+    )
     all_scans = exchange(1, scan_send.at[others], scan_recv.at[others], next_peer)
 
-    def send_slice(d, carry):
-        peer = lax.rem(me + d, seq_size)
-        exchange(0, state_send.at[peer], state_recv.at[me], peer).start()
-        return carry
-
-    lax.fori_loop(1, seq_size, send_slice, 0)
+    def each_peer(send):
+        send(lax.rem(me + seq_size // 2, seq_size))
+
+        def both_ways(d, carry):
+            send(lax.rem(me + seq_size // 2 + d, seq_size))
+            send(lax.rem(me + seq_size // 2 - d, seq_size))
+            return carry
+
+        lax.fori_loop(1, seq_size // 2, both_ways, 0)
+
+    def send_slice(peer):
+        exchange(0, state_send.at[peer, message], state_recv.at[me, message], peer).start()
+
+    each_peer(send_slice)
     state_recv[me] = state_send[me]
 
     blocks = [lax.rem(row + 2, 4), lax.rem(row + 1, 4), lax.rem(row + 3, 4), row]
@@ -185,12 +198,10 @@
 
     lax.fori_loop(0, seq_size, scan, jnp.zeros((slice_rows, HEAD_DIM), F32), unroll=4)
 
-    def send_scan(d, carry):
-        peer = lax.rem(me + d, seq_size)
+    def send_scan(peer):
         exchange(1, scan_send.at[peer], scan_recv.at[me], peer).start()
-        return carry
-
-    lax.fori_loop(1, seq_size, send_scan, 0)
+
+    each_peer(send_scan)
     scan_recv[me] = scan_send[me]
 
     inside(blocks[2])

time: 108 us -> 104 us (0.963)
  Pallas kernels: 106 us -> 102 us
    pallas_call x1, Pallas kernels: 106 us -> 102 us  [per_device(): pl.pallas_call(functools.partial(kernel, seq_size), out_shape=jax.ShapeDt...]
where the time goes in v3:
time: 104 us
  Pallas kernels  102 us (98%)
  local copies, waits for them, and re-layouts  2.29 us (2%)
    pallas_call x1, Pallas kernels, per_device(): pl.pallas_call(functools.partial(kernel, seq_size), out_shape=jax.ShapeDt...  102 us
    unnamed x1, local copies, waits for them, and re-layouts  2.29 us

profile of v3, /device:TPU:1, one launch (start us, length us, event | category | flops | bytes accessed | tf_op | source)
XLA Modules:
  0.0 103.9 jit_solution(13002913056868256850)
XLA Ops:
  0.0 101.6 %shard_map.64 = bf16[128,4096]{1,0:T(8,128)(2,1)} custom-call(f32[4,1024]{1,0:T(4,128)} %bitcast.1, bf16[1024,512]{1,0:T(8,128)(2,1)} %k_hbm.1, bf16[1024,512]{1,0:T(8,128)(2,1)} %v_hbm.1, bf16[1024,512]{1,0:T(8,128)(2,1)} %q_hbm.1, bf16[1024,512]{1,0:T(8,128)(2,1)} %g_hbm.1, bf16[512,4096]{1,0:T(8,128)(2,1)} %w_hbm.1), custom_call_target="tpu_custom_call" | custom-call | tf_op jit(solution)/shard_map/pallas_call | solution.py:330
  101.7 2.3 %copy.8 = bf16[128,4096]{1,0:T(8,128)(2,1)} copy(bf16[128,4096]{1,0:T(8,128)(2,1)} %shard_map.64) | data formatting | bytes 2097152

commit v4 on v3

--- a/solution.py
+++ b/solution.py
@@ -16,7 +16,10 @@
 WIDTH = 4096
 CHUNK = 512
 CHUNKS = WIDTH // CHUNK
-SIDE = CHUNKS // 2
+RING = CHUNKS // 2
+SIDE = RING // 2
+QUARTERS = CHUNKS - RING
+XS = 4
 F32 = jnp.float32
 BF16 = jnp.bfloat16
 MESH = pl.DeviceIdType.MESH
@@ -33,9 +36,10 @@
     rate, padded, k, v, q, g, w, w_send, w_recv, w_pair,
     run_col, run_row, start, lead, state_send, state_recv, scan_send, scan_recv,
     att, since, silu, entry, hid, hid_recv, far, plus, minus, own, far_recv, direct_recv,
-    sum_recv, result,
+    sum_recv, result, quarter, w_mate, hid_mate, pair_out, pair_in, pair_own,
     load_sem, a_send, a_recv, w_ssem, w_rsem, h_ssem, h_rsem,
-    y_send, y_recv, o_sem,
+    y_send, y_recv, o_sem, line_sem, q_send, q_recv, x_send, x_recv, d_send, d_recv,
+    m_send, m_recv, g_send, g_recv,
 ):
     me = lax.axis_index("seq")
     head = lax.axis_index("head")
@@ -46,6 +50,12 @@
     down = lax.rem(row + 3, 4) * 2 + core
     slice_rows = FEATURES // seq_size
     per_head = HEAD_DIM // slice_rows
+    odd = lax.rem(row, 2)
+    mate = (row + 1 - 2 * odd) * 2 + core
+    cross = lax.rem(row + 3 + 2 * odd, 4) * 2 + core
+    x = lax.rem(me, XS)
+    x_up = me - x + lax.rem(x + 1, XS)
+    x_down = me - x + lax.rem(x + 3, XS)
 
     loads = [
         pltpu.make_async_copy(src, dst, load_sem.at[i])
@@ -58,12 +68,15 @@
 
     barrier = pltpu.get_barrier_semaphore()
 
-    def greet(d, carry):
-        peer = lax.rem(me + d, seq_size)
+    def greet(peer):
         pl.semaphore_signal(barrier, inc=1, device_id=(peer, head), device_id_type=MESH)
-        return carry
-
-    lax.fori_loop(1, seq_size, greet, 0)
+
+    zs = seq_size // XS
+    x_line = [me - x + lax.rem(x + d, XS) for d in range(1, XS)]
+    for peer in x_line:
+        greet(peer)
+    for d in range(1, zs):
+        greet(lax.rem(me + d * XS, seq_size))
     for other in (partner, up, down):
         pl.semaphore_signal(barrier, inc=1, device_id=(me, other), device_id_type=MESH)
 
@@ -94,6 +107,9 @@
         lead[b] = jnp.broadcast_to(jnp.exp(ahead), (8, HEAD_DIM))
         ahead = ahead + totals[8 * b:8 * b + 8]
     through = jnp.broadcast_to(jnp.exp(ahead), (8, HEAD_DIM))
+    pl.semaphore_wait(barrier, XS - 1 + zs - 1 + 3)
+    for peer in x_line:
+        pl.semaphore_signal(line_sem, inc=1, device_id=(peer, head), device_id_type=MESH)
     loads[1].wait()
     loads[2].wait()
     for load in loads[3:]:
@@ -113,7 +129,7 @@
             through[h:h + 1], (per_head, 8, HEAD_DIM)
         )
 
-    pl.semaphore_wait(barrier, seq_size + 2)
+    pl.semaphore_wait(line_sem, XS - 1)
 
     def exchange(phase, src, dst, peer):
         return pltpu.make_async_remote_copy(
@@ -146,14 +162,55 @@
     state_recv[me] = state_send[me]
 
     blocks = [lax.rem(row + 2, 4), lax.rem(row + 1, 4), lax.rem(row + 3, 4), row]
-    order = [n // 2 + (n % 2) * SIDE for n in range(CHUNKS)]
+    order = [n // 2 + (n % 2) * SIDE for n in range(RING)]
 
     def columns(n):
         return slice(n * CHUNK, (n + 1) * CHUNK)
 
     loads[4].wait()
+
+    def remote(src, dst, send_sem, recv_sem, device):
+        return pltpu.make_async_remote_copy(
+            src_ref=src, dst_ref=dst, send_sem=send_sem, recv_sem=recv_sem,
+            device_id=device, device_id_type=MESH,
+        )
+
+    def paired_columns(part):
+        return pl.ds(pl.multiple_of((RING + part) * CHUNK, CHUNK), CHUNK)
+
+    deep = FEATURES // 2
+    quarter_copies = []
+    for i in range(2):
+        quarter[i] = w[i * deep:(i + 1) * deep, paired_columns(x)].astype(F32)
+        quarter_copies.append(
+            remote(quarter.at[i], w_mate.at[0, x, i], q_send.at[i], q_recv.at[i], (me, mate))
+        )
+        quarter_copies[-1].start()
+    parts = [x, lax.rem(x + 3, XS), lax.rem(x + 1, XS), lax.rem(x + 2, XS)]
+    x_copies = []
+    for i in range(2):
+        x_copies.append([
+            remote(
+                w_mate.at[0, x, i], w_mate.at[0, x, i], x_send.at[side, i], x_recv.at[side, i],
+                (peer, head),
+            )
+            for side, peer in ((0, x_up), (1, x_down))
+        ])
+    relay_up = remote(
+        w_mate.at[0, parts[1], 0], w_mate.at[0, parts[1], 0], x_send.at[0, 2], x_recv.at[0, 2],
+        (x_up, head),
+    )
+    relay_down = remote(
+        w_mate.at[0, parts[2], 1], w_mate.at[0, parts[2], 1], x_send.at[1, 2], x_recv.at[1, 2],
+        (x_down, head),
+    )
+    share_copies = [
+        remote(w_mate.at[0, part], w_mate.at[1, part], d_send.at[j], d_recv.at[j], (me, partner))
+        for j, part in enumerate(parts)
+    ]
+
     pair_copies = {}
-    for n in order:
+    for n in order + list(range(RING, CHUNKS)):
         w_send[n] = w[:, columns(n)].astype(F32)
         pair_copies[n] = pltpu.make_async_remote_copy(
             src_ref=w_send.at[n], dst_ref=w_recv.at[n],
@@ -206,8 +263,11 @@
 
     inside(blocks[2])
     inside(blocks[3])
-    for n in order[:SIDE]:
+    for n in order:
         receive_weights(n)
+    quarter_copies[0].wait_recv()
+    for copy in x_copies[0]:
+        copy.start()
     all_scans.wait_recv()
 
     hid_copies = []
@@ -252,70 +312,138 @@
         )
 
     far_copies = [
-        across(0, n, far.at[n], far_recv.at[n], up if n < SIDE else down) for n in range(CHUNKS)
+        across(0, n, far.at[n], far_recv.at[n], up if n < SIDE else down) for n in range(RING)
     ]
     direct_copies = [
         across(
             1, n, minus.at[n] if n < SIDE else plus.at[n], direct_recv.at[n],
             down if n < SIDE else up,
         )
-        for n in range(CHUNKS)
+        for n in range(RING)
     ]
     sum_copies = [
         across(
             2, n, plus.at[n] if n < SIDE else minus.at[n], sum_recv.at[n],
             up if n < SIDE else down,
         )
-        for n in range(CHUNKS)
+        for n in range(RING)
     ]
+    mate_turn, cross_turn = 1 + odd, 2 - odd
+    mate_copies = []
+    for block, t in enumerate((0, mate_turn)):
+        for i, src in enumerate((hid.at[t, core], hid_recv.at[t])):
+            mate_copies.append(
+                remote(
+                    src, hid_mate.at[block, i], m_send.at[block, i], m_recv.at[block, i], (me, mate)
+                )
+            )
+    cross_copies = [
+        remote(pair_out.at[j], pair_in.at[j], g_send.at[j], g_recv.at[j], (me, cross))
+        for j in range(QUARTERS)
+    ]
+
+    def paired(block, t, part):
+        products = (
+            (hid[t, core], w[:, paired_columns(part)]),
+            (hid_recv[t], w_recv[RING + part].astype(BF16)),
+            (hid_mate[block, 0], w_mate[0, part].reshape(FEATURES, CHUNK).astype(BF16)),
+            (hid_mate[block, 1], w_mate[1, part].reshape(FEATURES, CHUNK).astype(BF16)),
+        )
+        total = jnp.zeros((HALF, CHUNK), F32)
+        for left, right in products:
+            total += jnp.dot(left.astype(BF16), right, preferred_element_type=F32)
+        return total
+
+    def cross_out(j):
+        share_copies[j].wait_recv()
+        pair_out[j] = paired(0, cross_turn, parts[j])
+        cross_copies[j].start()
 
     hide(0)
     hid_copies[0].wait_recv()
-    for i, n in enumerate(order):
-        if i >= SIDE:
-            receive_weights(n)
+    for copy in mate_copies[:2]:
+        copy.start()
+    for n in order:
         far[n] = project(0, n)
         far_copies[n].start()
+    quarter_copies[1].wait_recv()
+    for copy in x_copies[1]:
+        copy.start()
+    share_copies[0].start()
     hide(1)
     hide(2)
     hid_copies[1].wait_recv()
-    for n in range(SIDE, CHUNKS):
+    for n in range(SIDE, RING):
         plus[n] = project(1, n)
         direct_copies[n].start()
     hid_copies[2].wait_recv()
     for n in range(SIDE):
         minus[n] = project(2, n)
         direct_copies[n].start()
+    for copy in mate_copies[2:]:
+        copy.start()
+    x_copies[0][0].wait_recv()
+    relay_up.start()
     for n in range(SIDE):
         plus[n] = project(1, n)
         minus[SIDE + n] = project(2, SIDE + n)
+    hide(3)
+    hid_copies[3].wait_recv()
+    for n in order:
+        own[n] = project(3, n)
+    for n in range(RING, CHUNKS):
+        pair_copies[n].wait_recv()
+    x_copies[0][1].wait_recv()
+    x_copies[1][1].wait_recv()
+    relay_down.start()
+    share_copies[2].start()
+    x_copies[1][0].wait_recv()
+    share_copies[1].start()
+    for copy in mate_copies[:2]:
+        copy.wait_recv()
+    cross_out(0)
+    for n in range(SIDE):
         far_copies[n].wait_recv()
         plus[n] += far_recv[n]
         sum_copies[n].start()
         far_copies[SIDE + n].wait_recv()
         minus[SIDE + n] += far_recv[SIDE + n]
         sum_copies[SIDE + n].start()
-    hide(3)
-    hid_copies[3].wait_recv()
-    for n in order:
-        own[n] = project(3, n)
+    cross_out(1)
+    cross_out(2)
+    relay_up.wait_recv()
+    relay_down.wait_recv()
+    share_copies[3].start()
+    cross_out(3)
     for n in order:
         direct_copies[n].wait_recv()
         own[n] += direct_recv[n]
+    for copy in mate_copies[2:]:
+        copy.wait_recv()
+    for j in range(QUARTERS):
+        pair_own[j] = paired(1, 3, parts[j])
     out_copies = []
-    for n in order:
+
+    def put(i, where, value):
+        result[:, where] = value.astype(BF16)
+        out_copies.append(
+            pltpu.make_async_copy(result.at[:, where], out_ref.at[:, where], o_sem.at[i])
+        )
+        out_copies[-1].start()
+
+    for j, n in enumerate(order):
+        cross_copies[j].wait_recv()
+        put(RING + j, paired_columns(parts[j]), pair_own[j] + pair_in[j])
         sum_copies[n].wait_recv()
-        result[:, columns(n)] = (own[n] + sum_recv[n]).astype(BF16)
-        out_copies.append(
-            pltpu.make_async_copy(
-                result.at[:, columns(n)], out_ref.at[:, columns(n)], o_sem.at[n]
-            )
-        )
-        out_copies[-1].start()
+        put(n, columns(n), own[n] + sum_recv[n])
 
     all_slices.wait_send()
     all_scans.wait_send()
     for copy in list(pair_copies.values()) + hid_copies + far_copies + direct_copies + sum_copies:
+        copy.wait_send()
+    for copy in quarter_copies + x_copies[0] + x_copies[1] + [relay_up, relay_down]:
+        copy.wait_send()
+    for copy in share_copies + mate_copies + cross_copies:
         copy.wait_send()
     for copy in out_copies:
         copy.wait()
@@ -342,7 +470,7 @@
             vmem((FEATURES, WIDTH), BF16),
             vmem((CHUNKS, FEATURES, CHUNK), F32),
             vmem((CHUNKS, FEATURES, CHUNK), F32),
-            vmem((FEATURES, WIDTH), BF16),
+            vmem((FEATURES, RING * CHUNK), BF16),
             vmem((BLOCKS, BLOCK, 8), F32),
             vmem((BLOCKS, 8, BLOCK), F32),
             vmem((BLOCKS, HEADS, HEAD_DIM, HEAD_DIM), F32),
@@ -357,19 +485,28 @@
             vmem((2, HEADS, HEAD_DIM, HEAD_DIM), BF16),
             vmem((BLOCKS, 2, HALF, FEATURES), F32),
             vmem((BLOCKS, HALF, FEATURES), F32),
-            vmem((CHUNKS, HALF, CHUNK), F32),
-            vmem((CHUNKS, HALF, CHUNK), F32),
-            vmem((CHUNKS, HALF, CHUNK), F32),
-            vmem((CHUNKS, HALF, CHUNK), F32),
-            vmem((CHUNKS, HALF, CHUNK), F32),
-            vmem((CHUNKS, HALF, CHUNK), F32),
-            vmem((CHUNKS, HALF, CHUNK), F32),
+            vmem((RING, HALF, CHUNK), F32),
+            vmem((RING, HALF, CHUNK), F32),
+            vmem((RING, HALF, CHUNK), F32),
+            vmem((RING, HALF, CHUNK), F32),
+            vmem((RING, HALF, CHUNK), F32),
+            vmem((RING, HALF, CHUNK), F32),
+            vmem((RING, HALF, CHUNK), F32),
             vmem((HALF, WIDTH), BF16),
+            vmem((2, FEATURES // 2, CHUNK), F32),
+            vmem((2, QUARTERS, 2, FEATURES // 2, CHUNK), F32),
+            vmem((2, 2, HALF, FEATURES), F32),
+            vmem((QUARTERS, HALF, CHUNK), F32),
+            vmem((QUARTERS, HALF, CHUNK), F32),
+            vmem((QUARTERS, HALF, CHUNK), F32),
             dma((6,)), dma((2,)), dma((2,)), dma((CHUNKS,)), dma((CHUNKS,)), dma((BLOCKS,)), dma((BLOCKS,)),
-            dma((3, CHUNKS)), dma((3, CHUNKS)), dma((CHUNKS,)),
+            dma((3, RING)), dma((3, RING)), dma((CHUNKS,)),
+            pltpu.SemaphoreType.REGULAR, dma((2,)), dma((2,)), dma((2, 3)), dma((2, 3)),
+            dma((QUARTERS,)), dma((QUARTERS,)), dma((2, 2)), dma((2, 2)),
+            dma((QUARTERS,)), dma((QUARTERS,)),
         ],
         compiler_params=pltpu.CompilerParams(
-            collective_id=0, has_side_effects=True, vmem_limit_bytes=62 * 1024 * 1024
+            collective_id=0, has_side_effects=True, vmem_limit_bytes=67043328
         ),
     )(log_decay.T, key_vectors, value_vectors, queries, gate_input, out_weight)
 

time: 104 us -> 94.6 us (0.910)
  Pallas kernels: 102 us -> 92.1 us
    pallas_call x1, Pallas kernels: 102 us -> 92.1 us  [per_device(): pl.pallas_call(functools.partial(kernel, seq_size), out_shape=jax.ShapeDt...]
where the time goes in v4:
time: 94.6 us; the launch traced here: 94.4 us
  Pallas kernels  92.1 us (97%)
  local copies, waits for them, and re-layouts  2.29 us (2%)
    pallas_call x1, Pallas kernels, per_device(): pl.pallas_call(functools.partial(kernel, seq_size), out_shape=jax.ShapeDt...  92.1 us
    unnamed x1, local copies, waits for them, and re-layouts  2.29 us

profile of v4, /device:TPU:1, one launch (start us, length us, event | category | flops | bytes accessed | tf_op | source)
XLA Modules:
  0.0 94.4 jit_solution(9531417149115569664)
XLA Ops:
  0.0 92.1 %shard_map.64 = bf16[128,4096]{1,0:T(8,128)(2,1)} custom-call(f32[4,1024]{1,0:T(4,128)} %bitcast.1, bf16[1024,512]{1,0:T(8,128)(2,1)} %k_hbm.1, bf16[1024,512]{1,0:T(8,128)(2,1)} %v_hbm.1, bf16[1024,512]{1,0:T(8,128)(2,1)} %q_hbm.1, bf16[1024,512]{1,0:T(8,128)(2,1)} %g_hbm.1, bf16[512,4096]{1,0:T(8,128)(2,1)} %w_hbm.1), custom_call_target="tpu_custom_call" | custom-call | tf_op jit(solution)/shard_map/pallas_call | solution.py:458
  92.1 2.3 %copy.8 = bf16[128,4096]{1,0:T(8,128)(2,1)} copy(bf16[128,4096]{1,0:T(8,128)(2,1)} %shard_map.64) | data formatting | bytes 2097152

commit v5 on v4

--- a/solution.py
+++ b/solution.py
@@ -36,9 +36,9 @@
     rate, padded, k, v, q, g, w, w_send, w_recv, w_pair,
     run_col, run_row, start, lead, state_send, state_recv, scan_send, scan_recv,
     att, since, silu, entry, hid, hid_recv, far, plus, minus, own, far_recv, direct_recv,
-    sum_recv, result, quarter, w_mate, hid_mate, pair_out, pair_in, pair_own,
+    sum_recv, quarter, w_mate, hid_mate, pair_out, pair_in, pair_own,
     load_sem, a_send, a_recv, w_ssem, w_rsem, h_ssem, h_rsem,
-    y_send, y_recv, o_sem, line_sem, q_send, q_recv, x_send, x_recv, d_send, d_recv,
+    y_send, y_recv, line_sem, q_send, q_recv, x_send, x_recv, d_send, d_recv,
     m_send, m_recv, g_send, g_recv,
 ):
     me = lax.axis_index("seq")
@@ -56,6 +56,9 @@
     x = lax.rem(me, XS)
     x_up = me - x + lax.rem(x + 1, XS)
     x_down = me - x + lax.rem(x + 3, XS)
+    half = lax.rem(me // XS, 2)
+    z_pair = me + XS * (1 - 2 * half)
+    halves = (half, 1 - half)
 
     loads = [
         pltpu.make_async_copy(src, dst, load_sem.at[i])
@@ -179,29 +182,33 @@
         return pl.ds(pl.multiple_of((RING + part) * CHUNK, CHUNK), CHUNK)
 
     deep = FEATURES // 2
-    quarter_copies = []
-    for i in range(2):
-        quarter[i] = w[i * deep:(i + 1) * deep, paired_columns(x)].astype(F32)
-        quarter_copies.append(
-            remote(quarter.at[i], w_mate.at[0, x, i], q_send.at[i], q_recv.at[i], (me, mate))
-        )
-        quarter_copies[-1].start()
+    rows = pl.ds(pl.multiple_of(half * deep, deep), deep)
+    quarter[...] = w[rows, paired_columns(x)].astype(F32)
+    quarter_copies = [
+        remote(quarter, w_mate.at[0, x, half], q_send.at[0], q_recv.at[0], (me, mate)),
+        remote(
+            w_mate.at[0, x, half], w_mate.at[0, x, half], q_send.at[1], q_recv.at[1],
+            (z_pair, head),
+        ),
+    ]
+    quarter_copies[0].start()
     parts = [x, lax.rem(x + 3, XS), lax.rem(x + 1, XS), lax.rem(x + 2, XS)]
     x_copies = []
     for i in range(2):
         x_copies.append([
             remote(
-                w_mate.at[0, x, i], w_mate.at[0, x, i], x_send.at[side, i], x_recv.at[side, i],
+                w_mate.at[0, x, halves[i]], w_mate.at[0, x, halves[i]], x_send.at[side, i],
+                x_recv.at[side, i],
                 (peer, head),
             )
             for side, peer in ((0, x_up), (1, x_down))
         ])
     relay_up = remote(
-        w_mate.at[0, parts[1], 0], w_mate.at[0, parts[1], 0], x_send.at[0, 2], x_recv.at[0, 2],
+        w_mate.at[0, parts[1], half], w_mate.at[0, parts[1], half], x_send.at[0, 2], x_recv.at[0, 2],
         (x_up, head),
     )
     relay_down = remote(
-        w_mate.at[0, parts[2], 1], w_mate.at[0, parts[2], 1], x_send.at[1, 2], x_recv.at[1, 2],
+        w_mate.at[0, parts[2], 1 - half], w_mate.at[0, parts[2], 1 - half], x_send.at[1, 2], x_recv.at[1, 2],
         (x_down, head),
     )
     share_copies = [
@@ -269,6 +276,7 @@
     for copy in x_copies[0]:
         copy.start()
     all_scans.wait_recv()
+    quarter_copies[1].start()
 
     hid_copies = []
 
@@ -422,20 +430,12 @@
         copy.wait_recv()
     for j in range(QUARTERS):
         pair_own[j] = paired(1, 3, parts[j])
-    out_copies = []
-
-    def put(i, where, value):
-        result[:, where] = value.astype(BF16)
-        out_copies.append(
-            pltpu.make_async_copy(result.at[:, where], out_ref.at[:, where], o_sem.at[i])
-        )
-        out_copies[-1].start()
 
     for j, n in enumerate(order):
         cross_copies[j].wait_recv()
-        put(RING + j, paired_columns(parts[j]), pair_own[j] + pair_in[j])
+        out_ref[:, paired_columns(parts[j])] = (pair_own[j] + pair_in[j]).astype(BF16)
         sum_copies[n].wait_recv()
-        put(n, columns(n), own[n] + sum_recv[n])
+        out_ref[:, columns(n)] = (own[n] + sum_recv[n]).astype(BF16)
 
     all_slices.wait_send()
     all_scans.wait_send()
@@ -445,8 +445,6 @@
         copy.wait_send()
     for copy in share_copies + mate_copies + cross_copies:
         copy.wait_send()
-    for copy in out_copies:
-        copy.wait()
 
 
 def per_device(seq_size, queries, key_vectors, value_vectors, gate_input, log_decay, out_weight):
@@ -457,9 +455,9 @@
     vmem = pltpu.VMEM
     return pl.pallas_call(
         functools.partial(kernel, seq_size),
-        out_shape=jax.ShapeDtypeStruct((HALF, WIDTH), BF16),
+        out_shape=pltpu.VMEM((HALF, WIDTH), BF16),
         in_specs=[whole] * 6,
-        out_specs=whole,
+        out_specs=pl.BlockSpec(memory_space=pltpu.VMEM),
         scratch_shapes=[
             vmem((HEADS, tokens), F32),
             vmem((BLOCKS, 8, BLOCK), F32),
@@ -492,21 +490,20 @@
             vmem((RING, HALF, CHUNK), F32),
             vmem((RING, HALF, CHUNK), F32),
             vmem((RING, HALF, CHUNK), F32),
-            vmem((HALF, WIDTH), BF16),
-            vmem((2, FEATURES // 2, CHUNK), F32),
+            vmem((FEATURES // 2, CHUNK), F32),
             vmem((2, QUARTERS, 2, FEATURES // 2, CHUNK), F32),
             vmem((2, 2, HALF, FEATURES), F32),
             vmem((QUARTERS, HALF, CHUNK), F32),
             vmem((QUARTERS, HALF, CHUNK), F32),
             vmem((QUARTERS, HALF, CHUNK), F32),
             dma((6,)), dma((2,)), dma((2,)), dma((CHUNKS,)), dma((CHUNKS,)), dma((BLOCKS,)), dma((BLOCKS,)),
-            dma((3, RING)), dma((3, RING)), dma((CHUNKS,)),
+            dma((3, RING)), dma((3, RING)),
             pltpu.SemaphoreType.REGULAR, dma((2,)), dma((2,)), dma((2, 3)), dma((2, 3)),
             dma((QUARTERS,)), dma((QUARTERS,)), dma((2, 2)), dma((2, 2)),
             dma((QUARTERS,)), dma((QUARTERS,)),
         ],
         compiler_params=pltpu.CompilerParams(
-            collective_id=0, has_side_effects=True, vmem_limit_bytes=67043328
+            collective_id=0, has_side_effects=True, vmem_limit_bytes=62 * 1024 * 1024
         ),
     )(log_decay.T, key_vectors, value_vectors, queries, gate_input, out_weight)
 

time: 94.6 us -> 91.8 us (0.970)
  Pallas kernels: 92.1 us -> 90.4 us
  local copies, waits for them, and re-layouts: 2.29 us -> 0.97 us
    pallas_call x1, Pallas kernels: 92.1 us -> 90.4 us  [per_device(): pl.pallas_call(functools.partial(kernel, seq_size), out_shape=pltpu.VMEM(...]
    unnamed x1, local copies, waits for them, and re-layouts: 2.29 us -> 0.97 us
where the time goes in v5:
time: 91.8 us; the launch traced here: 91.4 us
  Pallas kernels  90.4 us (98%)
  local copies, waits for them, and re-layouts  0.97 us (1%)
    pallas_call x1, Pallas kernels, per_device(): pl.pallas_call(functools.partial(kernel, seq_size), out_shape=pltpu.VMEM(...  90.4 us

profile of v5, /device:TPU:1, one launch (start us, length us, event | category | flops | bytes accessed | tf_op | source)
XLA Modules:
  0.0 91.4 jit_solution(7298061929679290356)
XLA Ops:
  0.0 90.4 %shard_map.64 = bf16[128,4096]{1,0:T(8,128)(2,1)S(1)} custom-call(f32[4,1024]{1,0:T(4,128)} %bitcast.1, bf16[1024,512]{1,0:T(8,128)(2,1)} %k_hbm.1, bf16[1024,512]{1,0:T(8,128)(2,1)} %v_hbm.1, bf16[1024,512]{1,0:T(8,128)(2,1)} %q_hbm.1, bf16[1024,512]{1,0:T(8,128)(2,1)} %g_hbm.1, bf16[512,4096]{1,0:T(8,128)(2,1)} %w_hbm.1), custom_call_target="tpu_custom_call" | custom-call | tf_op jit(solution)/shard_map/pallas_call | solution.py:456
  90.4 1.0 %copy.8 = bf16[128,4096]{1,0:T(8,128)(2,1)} copy(bf16[128,4096]{1,0:T(8,128)(2,1)S(1)} %shard_map.64) | data formatting | bytes 2097152

commit v6 on v5

--- a/solution.py
+++ b/solution.py
@@ -14,11 +14,11 @@
 BLOCKS = 4
 FEATURES = HEADS * HEAD_DIM
 WIDTH = 4096
-CHUNK = 512
-CHUNKS = WIDTH // CHUNK
-RING = CHUNKS // 2
+RING = 4
 SIDE = RING // 2
-QUARTERS = CHUNKS - RING
+CHUNK = 384
+QUARTERS = 4
+PAIRED = (WIDTH - RING * CHUNK) // QUARTERS
 XS = 4
 F32 = jnp.float32
 BF16 = jnp.bfloat16
@@ -33,7 +33,7 @@
 
 def kernel(
     seq_size, rate_hbm, k_hbm, v_hbm, q_hbm, g_hbm, w_hbm, out_ref,
-    rate, padded, k, v, q, g, w, w_send, w_recv, w_pair,
+    rate, padded, k, v, q, g, w, w_send, w_recv, p_send, p_recv, w_pair,
     run_col, run_row, start, lead, state_send, state_recv, scan_send, scan_recv,
     att, since, silu, entry, hid, hid_recv, far, plus, minus, own, far_recv, direct_recv,
     sum_recv, quarter, w_mate, hid_mate, pair_out, pair_in, pair_own,
@@ -179,7 +179,7 @@
         )
 
     def paired_columns(part):
-        return pl.ds(pl.multiple_of((RING + part) * CHUNK, CHUNK), CHUNK)
+        return pl.ds(pl.multiple_of(RING * CHUNK + part * PAIRED, HEAD_DIM), PAIRED)
 
     deep = FEATURES // 2
     rows = pl.ds(pl.multiple_of(half * deep, deep), deep)
@@ -217,14 +217,19 @@
     ]
 
     pair_copies = {}
-    for n in order + list(range(RING, CHUNKS)):
+    for n in order:
         w_send[n] = w[:, columns(n)].astype(F32)
-        pair_copies[n] = pltpu.make_async_remote_copy(
-            src_ref=w_send.at[n], dst_ref=w_recv.at[n],
-            send_sem=w_ssem.at[n], recv_sem=w_rsem.at[n],
-            device_id=(me, partner), device_id_type=MESH,
+        pair_copies[n] = remote(
+            w_send.at[n], w_recv.at[n], w_ssem.at[n], w_rsem.at[n], (me, partner)
         )
         pair_copies[n].start()
+    for part in range(QUARTERS):
+        p_send[part] = w[:, paired_columns(part)].astype(F32)
+        pair_copies[RING + part] = remote(
+            p_send.at[part], p_recv.at[part], w_ssem.at[RING + part], w_rsem.at[RING + part],
+            (me, partner),
+        )
+        pair_copies[RING + part].start()
 
     def receive_weights(n):
         pair_copies[n].wait_recv()
@@ -353,11 +358,11 @@
     def paired(block, t, part):
         products = (
             (hid[t, core], w[:, paired_columns(part)]),
-            (hid_recv[t], w_recv[RING + part].astype(BF16)),
-            (hid_mate[block, 0], w_mate[0, part].reshape(FEATURES, CHUNK).astype(BF16)),
-            (hid_mate[block, 1], w_mate[1, part].reshape(FEATURES, CHUNK).astype(BF16)),
-        )
-        total = jnp.zeros((HALF, CHUNK), F32)
+            (hid_recv[t], p_recv[part].astype(BF16)),
+            (hid_mate[block, 0], w_mate[0, part].reshape(FEATURES, PAIRED).astype(BF16)),
+            (hid_mate[block, 1], w_mate[1, part].reshape(FEATURES, PAIRED).astype(BF16)),
+        )
+        total = jnp.zeros((HALF, PAIRED), F32)
         for left, right in products:
             total += jnp.dot(left.astype(BF16), right, preferred_element_type=F32)
         return total
@@ -369,11 +374,11 @@
 
     hide(0)
     hid_copies[0].wait_recv()
-    for copy in mate_copies[:2]:
-        copy.start()
     for n in order:
         far[n] = project(0, n)
         far_copies[n].start()
+    for copy in mate_copies[:2]:
+        copy.start()
     quarter_copies[1].wait_recv()
     for copy in x_copies[1]:
         copy.start()
@@ -399,17 +404,6 @@
     hid_copies[3].wait_recv()
     for n in order:
         own[n] = project(3, n)
-    for n in range(RING, CHUNKS):
-        pair_copies[n].wait_recv()
-    x_copies[0][1].wait_recv()
-    x_copies[1][1].wait_recv()
-    relay_down.start()
-    share_copies[2].start()
-    x_copies[1][0].wait_recv()
-    share_copies[1].start()
-    for copy in mate_copies[:2]:
-        copy.wait_recv()
-    cross_out(0)
     for n in range(SIDE):
         far_copies[n].wait_recv()
         plus[n] += far_recv[n]
@@ -417,6 +411,17 @@
         far_copies[SIDE + n].wait_recv()
         minus[SIDE + n] += far_recv[SIDE + n]
         sum_copies[SIDE + n].start()
+    for part in range(QUARTERS):
+        pair_copies[RING + part].wait_recv()
+    for copy in mate_copies[:2]:
+        copy.wait_recv()
+    cross_out(0)
+    x_copies[0][1].wait_recv()
+    x_copies[1][1].wait_recv()
+    relay_down.start()
+    share_copies[2].start()
+    x_copies[1][0].wait_recv()
+    share_copies[1].start()
     cross_out(1)
     cross_out(2)
     relay_up.wait_recv()
@@ -466,8 +471,10 @@
             vmem((tokens, FEATURES), BF16),
             vmem((tokens, FEATURES), BF16),
             vmem((FEATURES, WIDTH), BF16),
-            vmem((CHUNKS, FEATURES, CHUNK), F32),
-            vmem((CHUNKS, FEATURES, CHUNK), F32),
+            vmem((RING, FEATURES, CHUNK), F32),
+            vmem((RING, FEATURES, CHUNK), F32),
+            vmem((QUARTERS, FEATURES, PAIRED), F32),
+            vmem((QUARTERS, FEATURES, PAIRED), F32),
             vmem((FEATURES, RING * CHUNK), BF16),
             vmem((BLOCKS, BLOCK, 8), F32),
             vmem((BLOCKS, 8, BLOCK), F32),
@@ -490,13 +497,13 @@
             vmem((RING, HALF, CHUNK), F32),
             vmem((RING, HALF, CHUNK), F32),
             vmem((RING, HALF, CHUNK), F32),
-            vmem((FEATURES // 2, CHUNK), F32),
-            vmem((2, QUARTERS, 2, FEATURES // 2, CHUNK), F32),
+            vmem((FEATURES // 2, PAIRED), F32),
+            vmem((2, QUARTERS, 2, FEATURES // 2, PAIRED), F32),
             vmem((2, 2, HALF, FEATURES), F32),
-            vmem((QUARTERS, HALF, CHUNK), F32),
-            vmem((QUARTERS, HALF, CHUNK), F32),
-            vmem((QUARTERS, HALF, CHUNK), F32),
-            dma((6,)), dma((2,)), dma((2,)), dma((CHUNKS,)), dma((CHUNKS,)), dma((BLOCKS,)), dma((BLOCKS,)),
+            vmem((QUARTERS, HALF, PAIRED), F32),
+            vmem((QUARTERS, HALF, PAIRED), F32),
+            vmem((QUARTERS, HALF, PAIRED), F32),
+            dma((6,)), dma((2,)), dma((2,)), dma((RING + QUARTERS,)), dma((RING + QUARTERS,)), dma((BLOCKS,)), dma((BLOCKS,)),
             dma((3, RING)), dma((3, RING)),
             pltpu.SemaphoreType.REGULAR, dma((2,)), dma((2,)), dma((2, 3)), dma((2, 3)),
             dma((QUARTERS,)), dma((QUARTERS,)), dma((2, 2)), dma((2, 2)),

time: 91.8 us -> 96.3 us (1.049)
  Pallas kernels: 90.4 us -> 95.2 us
    pallas_call x1, Pallas kernels: 90.4 us -> 95.2 us  [per_device(): pl.pallas_call(functools.partial(kernel, seq_size), out_shape=pltpu.VMEM(...]
where the time goes in v6:
time: 96.3 us; the launch traced here: 96.2 us
  Pallas kernels  95.2 us (99%)
  local copies, waits for them, and re-layouts  0.97 us (1%)
    pallas_call x1, Pallas kernels, per_device(): pl.pallas_call(functools.partial(kernel, seq_size), out_shape=pltpu.VMEM(...  95.2 us

profile of v6, /device:TPU:1, one launch (start us, length us, event | category | flops | bytes accessed | tf_op | source)
XLA Modules:
  0.0 96.2 jit_solution(15373659032218401880)
XLA Ops:
  0.0 95.2 %shard_map.64 = bf16[128,4096]{1,0:T(8,128)(2,1)S(1)} custom-call(f32[4,1024]{1,0:T(4,128)} %bitcast.1, bf16[1024,512]{1,0:T(8,128)(2,1)} %k_hbm.1, bf16[1024,512]{1,0:T(8,128)(2,1)} %v_hbm.1, bf16[1024,512]{1,0:T(8,128)(2,1)} %q_hbm.1, bf16[1024,512]{1,0:T(8,128)(2,1)} %g_hbm.1, bf16[512,4096]{1,0:T(8,128)(2,1)} %w_hbm.1), custom_call_target="tpu_custom_call" | custom-call | tf_op jit(solution)/shard_map/pallas_call | solution.py:461
  95.2 1.0 %copy.8 = bf16[128,4096]{1,0:T(8,128)(2,1)} copy(bf16[128,4096]{1,0:T(8,128)(2,1)S(1)} %shard_map.64) | data formatting | bytes 2097152

commit v7 on v5

--- a/solution.py
+++ b/solution.py
@@ -368,12 +368,12 @@
         cross_copies[j].start()
 
     hide(0)
+    mate_copies[0].start()
     hid_copies[0].wait_recv()
-    for copy in mate_copies[:2]:
-        copy.start()
     for n in order:
         far[n] = project(0, n)
         far_copies[n].start()
+    mate_copies[1].start()
     quarter_copies[1].wait_recv()
     for copy in x_copies[1]:
         copy.start()
@@ -399,6 +399,13 @@
     hid_copies[3].wait_recv()
     for n in order:
         own[n] = project(3, n)
+    for n in range(SIDE):
+        far_copies[n].wait_recv()
+        plus[n] += far_recv[n]
+        sum_copies[n].start()
+        far_copies[SIDE + n].wait_recv()
+        minus[SIDE + n] += far_recv[SIDE + n]
+        sum_copies[SIDE + n].start()
     for n in range(RING, CHUNKS):
         pair_copies[n].wait_recv()
     x_copies[0][1].wait_recv()
@@ -410,13 +417,6 @@
     for copy in mate_copies[:2]:
         copy.wait_recv()
     cross_out(0)
-    for n in range(SIDE):
-        far_copies[n].wait_recv()
-        plus[n] += far_recv[n]
-        sum_copies[n].start()
-        far_copies[SIDE + n].wait_recv()
-        minus[SIDE + n] += far_recv[SIDE + n]
-        sum_copies[SIDE + n].start()
     cross_out(1)
     cross_out(2)
     relay_up.wait_recv()

time: 91.8 us -> 93.2 us (1.015)
  Pallas kernels: 90.4 us -> 92 us
    pallas_call x1, Pallas kernels: 90.4 us -> 92 us  [per_device(): pl.pallas_call(functools.partial(kernel, seq_size), out_shape=pltpu.VMEM(...]
where the time goes in v7:
time: 93.2 us; the launch traced here: 93 us
  Pallas kernels  92 us (99%)
  local copies, waits for them, and re-layouts  0.97 us (1%)
    pallas_call x1, Pallas kernels, per_device(): pl.pallas_call(functools.partial(kernel, seq_size), out_shape=pltpu.VMEM(...  92 us

profile of v7, /device:TPU:1, one launch (start us, length us, event | category | flops | bytes accessed | tf_op | source)
XLA Modules:
  0.0 93.0 jit_solution(10026560776358123555)
XLA Ops:
  0.0 92.0 %shard_map.64 = bf16[128,4096]{1,0:T(8,128)(2,1)S(1)} custom-call(f32[4,1024]{1,0:T(4,128)} %bitcast.1, bf16[1024,512]{1,0:T(8,128)(2,1)} %k_hbm.1, bf16[1024,512]{1,0:T(8,128)(2,1)} %v_hbm.1, bf16[1024,512]{1,0:T(8,128)(2,1)} %q_hbm.1, bf16[1024,512]{1,0:T(8,128)(2,1)} %g_hbm.1, bf16[512,4096]{1,0:T(8,128)(2,1)} %w_hbm.1), custom_call_target="tpu_custom_call" | custom-call | tf_op jit(solution)/shard_map/pallas_call | solution.py:456
  92.0 1.0 %copy.8 = bf16[128,4096]{1,0:T(8,128)(2,1)} copy(bf16[128,4096]{1,0:T(8,128)(2,1)S(1)} %shard_map.64) | data formatting | bytes 2097152
